TPU v7x, 256 devices: a whole 4x4x8 slice. The times are simulated.
256 devices in a mesh: hb: 4 (over y), row: 16 (over z, x_hi), col: 4 (over x_lo, core).
Axes of the slice: x: 4 (x_hi: 2, x_lo: 2; x = x_hi * 2 + x_lo), y: 4, z: 8, core: 2. Of those that a mesh axis runs over, the one named last changes fastest.
Arguments:
- cell_state: float32 [256, 8, 256, 512], P('hb', None, 'row', 'col'), may hold values from -6 to 6
- normalizer: float32 [256, 8, 256], P('hb', None, 'row'), may hold values from 0.1 to 4
- stabilizer: float32 [256, 8, 16], P('hb', None, 'row'), may hold values from -5 to 120
- queries: float32 [256, 8, 256], P('hb', None, 'row'), may hold values from 0.0125 to 0.1125
- key_vectors: float32 [256, 8, 256], P('hb', None, 'row'), may hold values from -6 to 6
- token_value_vectors: float32 [256, 8, 512], P('hb', None, 'col'), may hold values from -6 to 6
- input_gate: float32 [256, 8], P('hb'), may hold values from -3 to 3
- forget_gate: float32 [256, 8], P('hb'), may hold values from -1 to 5
- output_gate_logits: float32 [256, 8, 512], P('hb', None, 'col'), may hold values from -6 to 6
- norm_gain: float32 [8, 512], P(None, 'col'), may hold values from 0.5 to 1.5
- out_weight: bfloat16 [8, 512, 4096], P('hb', 'col', 'row'), may hold values from -0.09375 to 0.09375
Outputs:
- layer_out: float32 [256, 4096], P('hb', 'row')
- readout: float32 [256, 8, 512], P('hb', None, 'col')
- refreshed_cell: float32 [256, 8, 256, 512], P('hb', None, 'row', 'col')
- new_normal: float32 [256, 8, 256], P('hb', None, 'row')
- new_stab: float32 [256, 8, 16], P('hb', None, 'row')
All inputs are finite; a program needn't handle non-finite values.
Results may differ from a plain program's by a relative error of at most 0.0029.
Values may be sent and summed in bfloat16 or wider, within the bound.
No kernel may reach another device: no remote copies, remote signals or barrier semaphores. Data moves between devices by JAX's collectives and lax.ppermute only.
A program may use at most 64 MiB of HBM per device.

v0:
```python
import jax
import jax.numpy as jnp
from jax import lax
from jax.sharding import Mesh
from jax.sharding import PartitionSpec as P

DK = 256
DV = 512
RBLK = 16
ROW = ("row_0", "row_1")


def all_in_one(x, axis):
    leaves = jax.tree.leaves(x)
    order = sorted(range(len(leaves)), key=lambda k: -leaves[k].size)
    width = (1, *leaves[order[0]].shape)[-1]
    lines = [
        jnp.pad(leaves[k].reshape(-1), (0, -leaves[k].size % width)).reshape(-1, width)
        for k in order
    ]
    both, at, found = (lax.all_gather(jnp.concatenate(lines), axis), 0, {})
    for k, line in zip(order, lines):
        share = both[:, at : at + len(line)].reshape(len(both), -1)
        found[k] = share[:, : leaves[k].size].reshape(-1, *leaves[k].shape)
        at += len(line)
    numbers = iter(range(len(leaves)))
    return jax.tree.map(lambda _: found[next(numbers)], x)


def combined_by_axis(x, axes, combine):
    for axis in axes:
        pieces = all_in_one(x, axis)
        x = jax.tree.map(lambda part: part[0], pieces)
        for k in range(1, lax.axis_size(axis)):
            x = combine(x, jax.tree.map(lambda part: part[k], pieces))
    return x


def sent_to_all(x, axis):
    copies = jnp.broadcast_to(x, (lax.axis_size(axis), *x.shape))
    return lax.all_to_all(copies, axis, split_axis=0, concat_axis=0, tiled=True)


def over_copies(x, axis):
    everything = sent_to_all(x, axis)
    return jnp.sum(everything, axis=0)


def together(arrays, axis):
    ends = [0]
    for a in arrays:
        ends.append(ends[-1] + a.size)
    running = over_copies(jnp.concatenate([a.ravel() for a in arrays]), axis)
    return tuple((running[b:e].reshape(a.shape) for a, b, e in zip(arrays, ends, ends[1:])))


def combine_pairs(left_pair, right_pair):
    joined = jnp.maximum(left_pair[0], right_pair[0])
    left_scale = jnp.exp(left_pair[0] - joined)
    right_scale = jnp.exp(right_pair[0] - joined)
    numerator = left_pair[1] * left_scale[:, :, None] + right_pair[1] * right_scale[:, :, None]
    denom = left_pair[2] * left_scale + right_pair[2] * right_scale
    return (joined, numerator, denom)


def local(
    cell_state,
    normalizer,
    stabilizer,
    queries,
    key_vectors,
    token_value_vectors,
    input_gate,
    forget_gate,
    output_gate_logits,
    norm_gain,
    out_weight,
):
    carried = jax.nn.log_sigmoid(forget_gate)[:, :, None] + stabilizer
    fresh = jnp.maximum(carried, input_gate[:, :, None])
    keep = jnp.repeat(jnp.exp(carried - fresh), RBLK, axis=2)
    admit = jnp.repeat(jnp.exp(input_gate[:, :, None] - fresh), RBLK, axis=2)
    scaled = key_vectors * DK ** (-0.5)
    refreshed_cell = (
        keep[:, :, :, None] * cell_state
        + (admit * scaled)[:, :, :, None] * token_value_vectors[:, :, None, :]
    )
    new_normal = keep * normalizer + admit * scaled
    local_top = jnp.max(fresh, axis=2)
    weight_matrix = jnp.repeat(jnp.exp(fresh - local_top[:, :, None]), RBLK, axis=2) * queries
    numerator = jnp.einsum(
        "bhkv,bhk->bhv", refreshed_cell, weight_matrix, precision=lax.Precision.HIGHEST
    )
    denom = jnp.sum(new_normal * weight_matrix, axis=2)
    top, numerator, denom = combined_by_axis((local_top, numerator, denom), ROW, combine_pairs)
    readout = numerator / jnp.maximum(jnp.abs(denom), jnp.exp(-top))[:, :, None]
    running_totals, squares = together(
        (jnp.sum(readout, axis=2), jnp.sum(readout * readout, axis=2)), "col"
    )
    mean = running_totals / DV
    var = squares / DV - mean * mean
    normed = (readout - mean[:, :, None]) * lax.rsqrt(var + 1e-06)[:, :, None]
    gated = (normed * norm_gain * jax.nn.sigmoid(output_gate_logits)).astype(jnp.bfloat16)
    seq_rows = gated.shape[0]
    out_cols = out_weight.shape[2]
    partial_value = jnp.dot(
        gated.reshape(seq_rows, -1),
        lax.all_gather(out_weight, "hb", axis=0, tiled=True).reshape(-1, out_cols),
        preferred_element_type=jnp.float32,
    )
    layer_out = over_copies(partial_value, "col")
    return (layer_out, readout, refreshed_cell, new_normal, fresh)


def solution(mesh):
    torus = Mesh(
        mesh.devices.reshape(mesh.shape["hb"], 8, 2, mesh.shape["col"]),
        ("hb", "row_0", "row_1", "col"),
    )
    in_specs = (
        P("hb", None, ROW, "col"),
        P("hb", None, ROW),
        P("hb", None, ROW),
        P("hb", None, ROW),
        P("hb", None, ROW),
        P("hb", None, "col"),
        P("hb", None),
        P("hb", None),
        P("hb", None, "col"),
        P(None, "col"),
        P("hb", "col", ROW),
    )
    out_specs = (
        P("hb", ROW),
        P("hb", None, "col"),
        P("hb", None, ROW, "col"),
        P("hb", None, ROW),
        P("hb", None, ROW),
    )
    return jax.shard_map(local, mesh=torus, in_specs=in_specs, out_specs=out_specs, check_vma=False)
```

profile of v0, /device:TPU:1, one launch (start us, length us, event | category | flops | bytes accessed | tf_op | source)
XLA Modules:
  0.0 107.4 jit_solution(9087296757668042198)
XLA Ops:
  7.2 0.0 all-gather.4.cloned.1.call-start
  7.2 0.7 fusion.24
  7.9 0.7 subtract_exponential_fusion.2
  8.6 0.0 copy-start.3
  8.6 0.1 copy.35
  8.7 0.7 exponential_multiply_fusion
  9.4 0.1 copy.33
  9.5 1.6 %multiply_reduce_fusion.1 = (f32[64,8]{0,1:T(8,128)S(1)}, f32[64,8,16]{0,2,1:T(8,128)}, f32[64,8,16]{0,2,1:T(8,128)S(1)}, f32[64,8,16,1]{0,2,1,3:T(8,128)S(1)}) fusion(f32[64,8,16]{0,2,1:T(8,128)} %param.14, f32[64,8]{0,1:T(8,128)S(1)} %bitcast.431, f32[64,8,16]{0,2,1:T(8,128)} %param.12, f32[64,8]{0,1:T(8,128)S(1)} %bitcast.426, f32[64,8,16]{0,2,1:T(8,128)} %param.15, ...), kind=kLoop, calls=%fused_computation.41 | loop fusion | flops 48640 | bytes 204800 | tf_op jit(solution)/shard_map/reduce_sum | solution.py:94
  11.1 0.1 copy.34
  11.2 0.1 copy.39
  11.4 0.1 copy.36
  11.5 0.1 reshape.563
  11.6 0.1 reshape.561
  11.6 4.0 %multiply_add_fusion = f32[64,8,16,128]{3,2,1,0:T(8,128)S(1)} fusion(f32[64,8,16,128]{3,2,1,0:T(8,128)} %param.11, f32[64,8,128]{2,1,0:T(8,128)} %param.16, f32[64,8,16]{2,1,0:T(8,128)S(1)} %copy.34, f32[64,8]{1,0:T(8,128)S(1)} %copy.33), kind=kLoop, calls=%fused_computation | loop fusion | flops 3145728 | bytes 8685568 | tf_op jit(solution)/shard_map/add | solution.py:85
  15.7 0.0 copy-done.3
  15.7 0.0 copy-start
  15.7 2.0 %copy-done = f32[64,8,16,128]{3,2,1,0:T(8,128)} copy-done((f32[64,8,16,128]{3,2,1,0:T(8,128)}, f32[64,8,16,128]{3,2,1,0:T(8,128)S(1)}, u32[]{:S(2)}) %copy-start) | copy-done | bytes 4194328
  17.7 4.0 %fusion.81 = f32[64,8,1,128]{3,2,1,0:T(1,128)S(1)} fusion(f32[64,8,16,128]{3,2,1,0:T(8,128)S(1)} %multiply_add_fusion, f32[64,8,16,1]{2,3,1,0:T(1,128)S(1)} %copy.39), kind=kOutput, calls=%fused_computation.160 | convolution fusion | flops 12582912 | bytes 4489216 | tf_op jit(solution)/shard_map/bhkv,bhk->bhv/dot_general | solution.py:91
  21.7 0.0 copy-start.1
  21.7 0.0 copy-start.4
  21.7 0.7 pad_maximum_fusion
  22.4 0.0 all-gather.4.cloned.1.call-update
  22.5 0.0 copy-done.2
  22.5 12.6 %all_gather.19 = bf16[8,128,256]{2,1,0:T(8,128)(2,1)S(1)} all-gather(bf16[2,128,256]{2,1,0:T(8,128)(2,1)S(1)} %copy-done.2), channel_id=1, replica_groups=mesh['hb'=4,'row_0'=8,'row_1'=2,'col'=4] {'hb'}, dimensions={0}, use_global_device_ids=true | all-gather | bytes 655360 | tf_op jit(solution)/shard_map/all_gather | solution.py:108
  35.1 27.9 %all-gather.4.cloned.1.call-done = f32[4160,128]{1,0:T(8,128)} async-done(((f32[520,128]{1,0:T(8,128)}), f32[4160,128]{1,0:T(8,128)}) %all-gather.4.cloned.1.call-update) | async-done | bytes 2129936 | tf_op jit(solution)/shard_map/all_gather | solution.py:21
  63.0 0.7 fusion.67
  63.7 0.8 fusion.28
  64.5 0.7 fusion.66
  65.2 0.7 fusion.64
  65.9 0.7 fusion.62
  66.6 2.5 %fusion.1 = f32[512,128]{1,0:T(8,128)S(1)} fusion(f32[8,520,128]{2,1,0:T(8,128)} %bitcast.423, f32[512]{0:T(512)S(1)} %get-tuple-element.37, f32[512]{0:T(512)S(1)} %get-tuple-element.34, f32[512]{0:T(512)S(1)} %get-tuple-element.36, f32[512]{0:T(512)S(1)} %get-tuple-element.35, f32[512]{0:T(512)S(1)} %get-tuple-element.33, f32[512]{0:T(512)S(1)} %get-tuple-element.31, ...), kind=kLoop, calls=%fused_computation.6 | loop fusion | flops 1376256 | bytes 2387968 | tf_op jit(solution)/shard_map/add | solution.py:61
  69.1 7.4 %all-gather.1 = f32[1040,128]{1,0:T(8,128)S(1)} all-gather(f32[520,128]{1,0:T(8,128)S(1)} %pad_maximum_fusion.1), channel_id=3, replica_groups=mesh['hb'=4,'row_0'=8,'row_1'=2,'col'=4] {'row_1'}, dimensions={0}, use_global_device_ids=true | all-gather | bytes 798720 | tf_op jit(solution)/shard_map/all_gather | solution.py:21
  76.6 0.4 fusion.78
  77.0 0.6 broadcast_in_dim.10
  77.6 9.4 %all-to-all-start = ((f32[4,1,1024]{2,1,0:T(1,128)}), f32[4,1,1024]{2,1,0:T(1,128)S(1)}, u32[]{:S(2)}, u32[]{:S(2)}) async-start(f32[4,1,1024]{2,1,0:T(1,128)} %broadcast_in_dim.10), calls=%async_computation | async-start | bytes 32768 | tf_op jit(solution)/shard_map/all_to_all | solution.py:41
  87.0 0.1 squeeze.147
  87.1 0.1 squeeze.148
  87.2 0.1 squeeze.150
  87.3 0.1 squeeze.151
  87.4 2.8 %all-to-all-done = f32[4,1,1024]{2,1,0:T(1,128)S(1)} async-done(((f32[4,1,1024]{2,1,0:T(1,128)}), f32[4,1,1024]{2,1,0:T(1,128)S(1)}, u32[]{:S(2)}, u32[]{:S(2)}) %all-to-all-start) | async-done | bytes 16416 | tf_op jit(solution)/shard_map/all_to_all | solution.py:41
  90.2 0.1 div.32
  90.3 0.1 div.34
  90.4 0.0 copy-done.1
  90.4 0.0 copy-done.4
  90.4 1.1 %multiply_convert_fusion = (bf16[64,8,128]{2,1,0:T(8,128)(2,1)S(1)}, f32[64,8,128]{2,1,0:T(8,128)}) fusion(f32[64,8,128]{2,1,0:T(8,128)S(1)} %copy-done.1, f32[8,128]{1,0:T(8,128)S(1)} %copy-done.4, f32[64,8]{1,0:T(8,128)S(1)} %get-tuple-element.53, f32[64,8]{1,0:T(8,128)S(1)} %div.32, f32[64,8]{1,0:T(8,128)S(1)} %get-tuple-element.47, ...), kind=kLoop, calls=%fused_computation.37 | loop fusion | flops 786432 | bytes 1193984 | tf_op jit(solution)/shard_map/convert_element_type | solution.py:103
  91.5 0.2 convolution_bitcast_fusion
  91.8 8.1 %all_to_all.11 = f32[4,64,256]{2,1,0:T(8,128)S(1)} all-to-all(f32[4,64,256]{2,1,0:T(8,128)S(1)} %broadcast_in_dim.11), channel_id=1, replica_groups=mesh['hb'=4,'row_0'=8,'row_1'=2,'col'=4] {'col'}, dimensions={0} | all-to-all | bytes 524288 | tf_op jit(solution)/shard_map/all_to_all | solution.py:41
  99.9 0.6 reduce_sum.49
  (9 shorter events, 0.1 us)
Async XLA Ops:
  7.2 55.8 %all-gather.4.cloned.1.call-start = ((), (), s32[]{:S(2)}) async-start(), calls=%async_computation.2 | async-start | bytes 2396160 | tf_op jit(solution)/shard_map/all_gather | solution.py:21
  8.6 7.0 %copy-start.3 = (f32[64,1,8]{0,2,1:T(8,128)}, f32[64,1,8]{0,2,1:T(8,128)S(1)}, u32[]{:S(2)}) copy-start(f32[64,1,8]{0,2,1:T(8,128)S(1)} %get-tuple-element.55) | copy-start | bytes 6148
  15.7 2.0 %copy-start = (f32[64,8,16,128]{3,2,1,0:T(8,128)}, f32[64,8,16,128]{3,2,1,0:T(8,128)S(1)}, u32[]{:S(2)}) copy-start(f32[64,8,16,128]{3,2,1,0:T(8,128)S(1)} %multiply_add_fusion) | copy-start | bytes 12582916
  17.7 4.8 %copy-start.2 = (bf16[2,128,256]{2,1,0:T(8,128)(2,1)S(1)}, bf16[2,128,256]{2,1,0:T(8,128)(2,1)}, u32[]{:S(2)}) copy-start(bf16[2,128,256]{2,1,0:T(8,128)(2,1)} %param.21) | copy-start | bytes 393220
  21.7 68.7 %copy-start.1 = (f32[64,8,128]{2,1,0:T(8,128)S(1)}, f32[64,8,128]{2,1,0:T(8,128)}, u32[]{:S(2)}) copy-start(f32[64,8,128]{2,1,0:T(8,128)} %param.19) | copy-start | bytes 786436
  21.7 68.7 %copy-start.4 = (f32[8,128]{1,0:T(8,128)S(1)}, f32[8,128]{1,0:T(8,128)}, u32[]{:S(2)}) copy-start(f32[8,128]{1,0:T(8,128)} %param.20) | copy-start | bytes 12292
  77.6 12.5 %all-to-all-start = ((f32[4,1,1024]{2,1,0:T(1,128)}), f32[4,1,1024]{2,1,0:T(1,128)S(1)}, u32[]{:S(2)}, u32[]{:S(2)}) async-start(f32[4,1,1024]{2,1,0:T(1,128)} %broadcast_in_dim.10), calls=%async_computation | async-start | bytes 32768 | tf_op jit(solution)/shard_map/all_to_all | solution.py:41
Sparse Core Ops, SparseCore 0:
  22.6 40.3 all-gather.3
where the time goes:
time: 108 us; the launch traced here: 107 us
  waiting for transfers between devices  30.7 us (28%)
  blocking collectives  28.1 us (26%)
  other arithmetic  16.8 us (16%)
  between operations  14.2 us (13%)
  starting transfers between devices  9.42 us (9%)
  matrix products  4.21 us (4%)
  local copies, waits for them, and re-layouts  3.9 us (4%)
    all_gather x1, waiting for transfers between devices, all_in_one(): both, at, found = (lax.all_gather(jnp.concatenate(lines), axis), 0, {})  27.9 us
    all_gather x1, blocking collectives, local(): lax.all_gather(out_weight, 'hb', axis=0, tiled=True).reshape(-1, out_cols)  12.6 us
    all_to_all x1, starting transfers between devices, sent_to_all(): return lax.all_to_all(copies, axis, split_axis=0, concat_axis=0, tiled=True)  9.38 us
    all_to_all x1, blocking collectives, sent_to_all(): return lax.all_to_all(copies, axis, split_axis=0, concat_axis=0, tiled=True)  8.09 us
    all_gather x1, blocking collectives, all_in_one(): both, at, found = (lax.all_gather(jnp.concatenate(lines), axis), 0, {})  7.44 us
    add x1, other arithmetic, local(): keep[:, :, :, None] * cell_state  4.01 us
    dot_general x1, matrix products, local(): jnp.einsum('bhkv,bhk->bhv', refreshed_cell, weight_matrix, precision=lax....  4.01 us
    all_to_all x1, waiting for transfers between devices, sent_to_all(): return lax.all_to_all(copies, axis, split_axis=0, concat_axis=0, tiled=True)  2.76 us
  transfers between devices with their start and end apart: 2, of which 2 were waited for; matrix products, arithmetic and copies ran while one was open for 0% of the time, Pallas kernels for 0%

commit v1 on v0

v1 whole, which is shorter than its diff:
```python
import jax
import jax.numpy as jnp
from jax import lax
from jax.experimental import pallas as pl
from jax.experimental.pallas import tpu as pltpu
from jax.sharding import Mesh
from jax.sharding import PartitionSpec as P

H = 8
DK = 256
DV = 512
HB = 4
ROWS = 16
COLS = 4
B = 64
KR = 16
V = 128
OUT = 256
MINE = B // ROWS
NROWS = MINE * H
CHUNK = NROWS + H
NSCALE = 2048.0
DSCALE = 64.0
STEP = 256.0
f32 = jnp.float32
bf16 = jnp.bfloat16
f16 = jnp.float16


def whole(shape):
    return pl.BlockSpec(shape, lambda *_: (0,) * len(shape))


def parts_of(x):
    first = x.astype(bf16).astype(f32)
    rest = (x - first) * STEP
    second = rest.astype(bf16).astype(f32)
    third = (rest - second) * STEP
    return first, second, third


def cell_kernel(
    cell, normal, stab, query, keys, value, in_gate, forget, new_cell, new_normal, new_stab, send,
    keep_s, admit_s, denom_s, numer_s,
):
    h = pl.program_id(0)

    @pl.when(h == 0)
    def _():
        pre = forget[...]
        log_sig = jnp.minimum(pre, 0.0) - jnp.log(1.0 + jnp.exp(-jnp.abs(pre)))
        carried = log_sig + stab[...]
        fresh = jnp.maximum(carried, in_gate[...])
        new_stab[...] = fresh
        keep_s[...] = jnp.exp(carried - fresh)
        admit_s[...] = jnp.exp(in_gate[...] - fresh)

    row = pl.ds(h, 1)
    keep = jnp.broadcast_to(keep_s[row, :], (KR, B))
    add = jnp.broadcast_to(admit_s[row, :], (KR, B)) * (keys[h] * DK**-0.5)
    q = query[h]
    normed = keep * normal[h] + add
    new_normal[h] = normed
    denom_s[row, :] = jnp.sum(q * normed, axis=0, keepdims=True)
    for b in range(B):
        lane = slice(b, b + 1)
        v = jnp.broadcast_to(value[b, row, :], (KR, V))
        fresh_cell = keep[:, lane] * cell[b, 0] + add[:, lane] * v
        new_cell[b, 0] = fresh_cell
        numer_s[b, row, :] = jnp.sum(q[:, lane] * fresh_cell, axis=0, keepdims=True)

    @pl.when(h == H - 1)
    def _():
        fields = parts_of(new_stab[...]) + parts_of(denom_s[...] * DSCALE)
        wide = [jnp.concatenate([x, x], axis=1) for x in fields]
        lanes = lax.broadcasted_iota(jnp.int32, (H, 2 * B), 1)
        for r in range(ROWS):
            tile = jnp.zeros((H, 2 * B), f32)
            for n, x in enumerate(wide):
                shift = (MINE * n - MINE * r) % (2 * B)
                moved = pltpu.roll(x, shift, 1) if shift else x
                inside = (lanes >= MINE * n) & (lanes < MINE * (n + 1))
                tile = jnp.where(inside, moved, tile)
            send[r, NROWS:CHUNK, :] = tile
            for j in range(MINE):
                send[r, H * j : H * (j + 1), :] = numer_s[MINE * r + j] * NSCALE


def combine_kernel(got, out):
    def field(tile, n):
        back = lambda k: pltpu.roll(tile, (-MINE * k) % V, 1) if k else tile
        return back(n) + (back(n + 1) + back(n + 2) * (1.0 / STEP)) * (1.0 / STEP)

    tiles = [got[r, NROWS:CHUNK, :] for r in range(ROWS)]
    stabs = [field(t, 0) for t in tiles]
    top = stabs[0]
    for s in stabs[1:]:
        top = jnp.maximum(top, s)
    scales = [jnp.exp(s - top) for s in stabs]
    denom = scales[0] * field(tiles[0], 3)
    for s, t in zip(scales[1:], tiles[1:]):
        denom = denom + s * field(t, 3)
    base = jnp.maximum(jnp.abs(denom * (1.0 / DSCALE)), jnp.exp(-top)) * NSCALE
    for j in range(MINE):
        lane = slice(j, j + 1)
        rows = slice(H * j, H * (j + 1))
        numer = scales[0][:, lane] * got[0, rows, :]
        for r in range(1, ROWS):
            numer = numer + scales[r][:, lane] * got[r, rows, :]
        readout = (numer / jnp.broadcast_to(base[:, lane], (H, V))).astype(bf16)
        for r in range(ROWS):
            out[r, rows, :] = readout


def stats_kernel(got, readout, stats):
    lanes = lax.broadcasted_iota(jnp.int32, (H, 2 * B), 1)
    tile = jnp.zeros((H, 2 * B), f32)
    for b in range(B):
        x = got[b * H : (b + 1) * H, :].astype(f32)
        readout[b] = x
        total = jnp.sum(x, axis=1, keepdims=True)
        square = jnp.sum(x * x, axis=1, keepdims=True)
        tile = jnp.where(lanes == b, total, tile)
        tile = jnp.where(lanes == B + b, square, tile)
    stats[...] = tile


def project_kernel(me, readout, s0, s1, s2, s3, logits, gain, w0, w1, w2, w3, out, gated):
    total = (s0[...] + s1[...]) + (s2[...] + s3[...])
    mean = total[:, :B] * (1.0 / DV)
    square = total[:, B:] * (1.0 / DV)
    scale = lax.rsqrt(square - mean * mean + 1e-06)
    g = gain[...]
    for b in range(B):
        lane = slice(b, b + 1)
        gate = g / (1.0 + jnp.exp(-logits[b]))
        gated[b * H : (b + 1) * H, :] = (readout[b] - mean[:, lane]) * scale[:, lane] * gate
    acc = jnp.zeros((B, OUT), f32)
    for k, w in enumerate((w0, w1, w2, w3)):
        for j in range(H // HB):
            head = 2 * (me[0] ^ k) + j
            x = gated[pl.ds(head, B, stride=H), :]
            high = x.astype(bf16)
            low = (x - high.astype(f32)).astype(bf16)
            acc = acc + jnp.dot(high, w[j], preferred_element_type=f32)
            acc = acc + jnp.dot(low, w[j], preferred_element_type=f32)
    out[...] = acc


def xor_pairs(n, k):
    return [(i, i ^ k) for i in range(n)]


def local(
    cell_state,
    normalizer,
    stabilizer,
    queries,
    key_vectors,
    token_value_vectors,
    input_gate,
    forget_gate,
    output_gate_logits,
    norm_gain,
    out_weight,
):
    shape = jax.ShapeDtypeStruct
    weights = [out_weight] + [
        lax.ppermute(out_weight, "hb", xor_pairs(HB, k)) for k in range(1, HB)
    ]
    turned = lambda x: jnp.transpose(x, (1, 2, 0))
    cell_block = pl.BlockSpec((B, 1, KR, V), lambda h: (0, h, 0, 0))
    new_cell, new_normal, new_stab, send = pl.pallas_call(
        cell_kernel,
        grid=(H,),
        in_specs=[
            cell_block,
            whole((H, KR, B)),
            whole((H, B)),
            whole((H, KR, B)),
            whole((H, KR, B)),
            whole((B, H, V)),
            whole((H, B)),
            whole((H, B)),
        ],
        out_specs=[cell_block, whole((H, KR, B)), whole((H, B)), whole((ROWS, CHUNK, V))],
        out_shape=[
            shape((B, H, KR, V), f32),
            shape((H, KR, B), f32),
            shape((H, B), f32),
            shape((ROWS, CHUNK, V), f32),
        ],
        scratch_shapes=[
            pltpu.VMEM((H, B), f32),
            pltpu.VMEM((H, B), f32),
            pltpu.VMEM((H, B), f32),
            pltpu.VMEM((B, H, V), f32),
        ],
        name="cell",
    )(
        cell_state,
        turned(normalizer),
        jnp.transpose(stabilizer[:, :, 0]),
        turned(queries),
        turned(key_vectors),
        token_value_vectors,
        jnp.transpose(input_gate),
        jnp.transpose(forget_gate),
    )
    got = lax.all_to_all(send.astype(f16), "row", 0, 0, tiled=True).astype(f32)
    mine = pl.pallas_call(
        combine_kernel, out_shape=shape((ROWS, NROWS, V), bf16), name="combine"
    )(got)
    every = lax.all_to_all(mine, "row", 0, 0, tiled=True)
    readout, stats = pl.pallas_call(
        stats_kernel, out_shape=[shape((B, H, V), f32), shape((H, 2 * B), f32)], name="stats"
    )(every.reshape(B * H, V))
    others = [lax.ppermute(stats, "col", xor_pairs(COLS, k)) for k in range(1, COLS)]
    me = lax.axis_index("hb").astype(jnp.int32).reshape(1)
    vmem = pl.BlockSpec(memory_space=pltpu.VMEM)
    partial_value = pl.pallas_call(
        project_kernel,
        in_specs=[pl.BlockSpec(memory_space=pltpu.SMEM)] + [vmem] * 11,
        out_specs=vmem,
        out_shape=shape((B, OUT), f32),
        scratch_shapes=[pltpu.VMEM((B * H, V), f32)],
        name="project",
    )(me, readout, stats, *others, output_gate_logits, norm_gain, *weights)
    sent = [lax.ppermute(partial_value, "col", xor_pairs(COLS, k)) for k in range(1, COLS)]
    layer_out = (partial_value + sent[0]) + (sent[1] + sent[2])
    return (
        layer_out,
        readout,
        new_cell,
        jnp.transpose(new_normal, (2, 0, 1)),
        jnp.transpose(new_stab)[:, :, None],
    )


def solution(mesh):
    in_specs = (
        P("hb", None, "row", "col"),
        P("hb", None, "row"),
        P("hb", None, "row"),
        P("hb", None, "row"),
        P("hb", None, "row"),
        P("hb", None, "col"),
        P("hb", None),
        P("hb", None),
        P("hb", None, "col"),
        P(None, "col"),
        P("hb", "col", "row"),
    )
    out_specs = (
        P("hb", "row"),
        P("hb", None, "col"),
        P("hb", None, "row", "col"),
        P("hb", None, "row"),
        P("hb", None, "row"),
    )
    return jax.shard_map(local, mesh=mesh, in_specs=in_specs, out_specs=out_specs, check_vma=False)
```

time: 108 us -> 69.6 us (0.64)
  waiting for transfers between devices: 30.7 us -> 11.9 us
  Pallas kernels: 0 us -> 15.6 us
  other arithmetic: 16.8 us -> 3.24 us
  between operations: 14.2 us -> 0.72 us
  blocking collectives: 28.1 us -> 21.6 us
  starting transfers between devices: 9.42 us -> 14.8 us
  matrix products: 4.21 us -> 0 us
  local copies, waits for them, and re-layouts: 3.9 us -> 1.23 us
    all_gather x1 -> x0, waiting for transfers between devices: 27.9 us -> none  [all_in_one(): both, at, found = (lax.all_gather(jnp.concatenate(lines), axis), 0, {})]
    all_gather x2 -> x0, blocking collectives: 20 us -> none  [the longest x1 12.6 us: local(): lax.all_gather(out_weight, 'hb', axis=0, tiled=True).reshape(-1, out_cols)]
    pallas_call x0 -> x4, Pallas kernels: none -> 15.6 us  [the longest x1 9.52 us: local(): pl.pallas_call(cell_kernel, grid=(H,), in_specs=[cell_block, whole((H, KR...]
    all_to_all x1, blocking collectives: 8.09 us -> 21.6 us  [local(): got = lax.all_to_all(send.astype(f16), 'row', 0, 0, tiled=True).astype(f32)]
    ppermute x0 -> x9, starting transfers between devices: none -> 11.3 us  [the longest x3 5.11 us: local(): lax.ppermute(stats, 'col', xor_pairs(COLS, k))]
    all_to_all x1, starting transfers between devices: 9.38 us -> 3.51 us  [local(): every = lax.all_to_all(mine, 'row', 0, 0, tiled=True)]
    add x3 -> x1, other arithmetic: 7.32 us -> 1.49 us  [local(): layer_out = partial_value + sent[0] + (sent[1] + sent[2])]
    ppermute x0 -> x9, waiting for transfers between devices: none -> 5.71 us  [the longest x3 3.82 us: local(): lax.ppermute(partial_value, 'col', xor_pairs(COLS, k))]
  transfers between devices with their start and end apart: 2 -> 10, of which waited for: 2 -> 5; matrix products, arithmetic and copies ran while one was open for 0% -> 0% of each run, Pallas kernels for 0% -> 2%
where the time goes in v1:
time: 69.6 us; the launch traced here: 69.1 us
  blocking collectives  21.6 us (31%)
  Pallas kernels  15.6 us (22%)
  starting transfers between devices  14.8 us (21%)
  waiting for transfers between devices  11.9 us (17%)
  other arithmetic  3.24 us (5%)
  local copies, waits for them, and re-layouts  1.23 us (2%)
  between operations  0.72 us (1%)
    all_to_all x1, blocking collectives, local(): got = lax.all_to_all(send.astype(f16), 'row', 0, 0, tiled=True).astype(f32)  21.6 us
    pallas_call x1, Pallas kernels, local(): pl.pallas_call(cell_kernel, grid=(H,), in_specs=[cell_block, whole((H, KR...  9.52 us
    all_to_all x1, waiting for transfers between devices, local(): every = lax.all_to_all(mine, 'row', 0, 0, tiled=True)  6.16 us
    ppermute x3, starting transfers between devices, local(): lax.ppermute(stats, 'col', xor_pairs(COLS, k))  5.11 us
    ppermute x3, starting transfers between devices, local(): lax.ppermute(out_weight, 'hb', xor_pairs(HB, k))  4.01 us
    ppermute x3, waiting for transfers between devices, local(): lax.ppermute(partial_value, 'col', xor_pairs(COLS, k))  3.82 us
    all_to_all x1, starting transfers between devices, local(): every = lax.all_to_all(mine, 'row', 0, 0, tiled=True)  3.51 us
    pallas_call x1, Pallas kernels, local(): pl.pallas_call(project_kernel, in_specs=[pl.BlockSpec(memory_space=pltpu....  2.47 us
  transfers between devices with their start and end apart: 10, of which 5 were waited for; matrix products, arithmetic and copies ran while one was open for 0% of the time, Pallas kernels for 2%

profile of v1, /device:TPU:1, one launch (start us, length us, event | category | flops | bytes accessed | tf_op | source)
XLA Modules:
  0.0 69.1 jit_solution(2623992047817808735)
XLA Ops:
  0.6 0.0 copy-start.1
  0.6 9.5 %cell.2 = (f32[64,8,16,128]{3,2,1,0:T(8,128)}, f32[8,16,64]{2,1,0:T(8,128)}, f32[8,64]{1,0:T(8,128)}, f32[16,40,128]{2,1,0:T(8,128)}) custom-call(f32[64,8,16,128]{3,2,1,0:T(8,128)} %cell.3, f32[8,16,64]{2,1,0:T(8,128)} %bitcast.17, f32[8,64]{1,0:T(8,128)} %bitcast.20, f32[8,16,64]{2,1,0:T(8,128)} %bitcast.18, f32[8,16,64]{2,1,0:T(8,128)} %bitcast.19, ...), custom_call_target="tpu_custom_call" | custom-call | tf_op jit(solution)/shard_map/cell/pallas_call | solution.py:173
  10.2 1.0 %convert_element_type.6 = f16[16,40,128]{2,1,0:T(8,128)(2,1)S(1)} convert(f32[16,40,128]{2,1,0:T(8,128)} %get-tuple-element.11) | non-fusion elementwise | flops 81920 | bytes 491520 | tf_op jit(solution)/shard_map/convert_element_type | solution.py:210
  11.2 21.6 %all_to_all.10 = f16[16,40,128]{2,1,0:T(8,128)(2,1)S(1)} all-to-all(f16[16,40,128]{2,1,0:T(8,128)(2,1)S(1)} %convert_element_type.6), channel_id=1, replica_groups=mesh['hb'=4,'row'=16,'col'=4] {'row'}, dimensions={0} | all-to-all | bytes 327680 | tf_op jit(solution)/shard_map/all_to_all | solution.py:210
  32.8 0.8 %convert_element_type.7.got = f32[16,40,128]{2,1,0:T(8,128)} convert(f16[16,40,128]{2,1,0:T(8,128)(2,1)S(1)} %all_to_all.10) | non-fusion elementwise | flops 81920 | bytes 491520 | tf_op jit(solution)/shard_map/convert_element_type | solution.py:210
  33.6 1.9 %combine.1 = bf16[16,32,128]{2,1,0:T(8,128)(2,1)} custom-call(f32[16,40,128]{2,1,0:T(8,128)} %convert_element_type.7.got), custom_call_target="tpu_custom_call" | custom-call | tf_op jit(solution)/shard_map/combine/pallas_call | solution.py:211
  35.5 3.5 %all-to-all-start.1 = ((bf16[16,32,128]{2,1,0:T(8,128)(2,1)}), bf16[16,32,128]{2,1,0:T(8,128)(2,1)S(1)}, u32[]{:S(2)}, u32[]{:S(2)}) async-start(bf16[16,32,128]{2,1,0:T(8,128)(2,1)} %combine.1), calls=%async_computation.1 | async-start | bytes 262144 | tf_op jit(solution)/shard_map/all_to_all | solution.py:214
  39.0 0.0 copy-done.1
  39.0 1.4 %collective-permute-start.3 = (bf16[2,128,256]{2,1,0:T(8,128)(2,1)S(1)}, bf16[2,128,256]{2,1,0:T(8,128)(2,1)S(1)}, u32[]{:S(2)}, u32[]{:S(2)}) collective-permute-start(bf16[2,128,256]{2,1,0:T(8,128)(2,1)S(1)} %copy-done.1), channel_id=1, source_target_pairs={{0,64},{64,0},{128,192},{192,128},{1,65},{65,1},{129,193},{193,129... | collective-permute-start | bytes 393224 | tf_op jit(solution)/shard_map/ppermute | solution.py:169
  40.4 2.6 %collective-permute-start.4 = (bf16[2,128,256]{2,1,0:T(8,128)(2,1)S(1)}, bf16[2,128,256]{2,1,0:T(8,128)(2,1)S(1)}, u32[]{:S(2)}, u32[]{:S(2)}) collective-permute-start(bf16[2,128,256]{2,1,0:T(8,128)(2,1)S(1)} %copy-done.1), channel_id=1, source_target_pairs={{0,128},{64,192},{128,0},{192,64},{1,129},{65,193},{129,1},{193,65... | collective-permute-start | bytes 393224 | tf_op jit(solution)/shard_map/ppermute | solution.py:169
  43.0 0.0 collective-permute-start.5
  43.0 6.2 %all-to-all-done.1 = bf16[16,32,128]{2,1,0:T(8,128)(2,1)S(1)} async-done(((bf16[16,32,128]{2,1,0:T(8,128)(2,1)}), bf16[16,32,128]{2,1,0:T(8,128)(2,1)S(1)}, u32[]{:S(2)}, u32[]{:S(2)}) %all-to-all-start.1) | async-done | bytes 131104 | tf_op jit(solution)/shard_map/all_to_all | solution.py:214
  49.2 0.0 copy-start
  49.2 0.6 copy-done
  49.8 1.7 %stats.1 = (f32[64,8,128]{2,1,0:T(8,128)}, f32[8,128]{1,0:T(8,128)}) custom-call(bf16[512,128]{1,0:T(8,128)(2,1)} %bitcast.16), custom_call_target="tpu_custom_call" | custom-call | tf_op jit(solution)/shard_map/stats/pallas_call | solution.py:215
  51.5 3.5 %collective-permute-start = (f32[8,128]{1,0:T(8,128)}, f32[8,128]{1,0:T(8,128)S(1)}, u32[]{:S(2)}, u32[]{:S(2)}) collective-permute-start(f32[8,128]{1,0:T(8,128)} %get-tuple-element.13.s0), channel_id=1, source_target_pairs={{0,1},{1,0},{2,3},{3,2},{4,5},{5,4},{6,7},{7,6},{8,9},{9,8},{10,11... | collective-permute-start | bytes 12296 | tf_op jit(solution)/shard_map/ppermute | solution.py:218
  55.0 0.3 collective-permute-start.1
  55.3 0.0 collective-permute-done.3.w1
  55.3 0.0 copy-start.2
  55.3 1.3 %collective-permute-start.2 = (f32[8,128]{1,0:T(8,128)}, f32[8,128]{1,0:T(8,128)S(1)}, u32[]{:S(2)}, u32[]{:S(2)}) collective-permute-start(f32[8,128]{1,0:T(8,128)} %get-tuple-element.13.s0), channel_id=1, source_target_pairs={{0,3},{1,2},{2,1},{3,0},{4,7},{5,6},{6,5},{7,4},{8,11},{9,10},{10,... | collective-permute-start | bytes 12296 | tf_op jit(solution)/shard_map/ppermute | solution.py:218
  56.7 0.0 collective-permute-done.4.w2
  56.7 0.0 copy-start.3
  56.7 0.0 collective-permute-done.5.w3
  56.7 0.0 copy-start.4
  56.7 0.0 collective-permute-done.s1
  56.7 0.0 copy-start.5
  56.7 1.0 %collective-permute-done.1.s2 = f32[8,128]{1,0:T(8,128)S(1)} collective-permute-done((f32[8,128]{1,0:T(8,128)}, f32[8,128]{1,0:T(8,128)S(1)}, u32[]{:S(2)}, u32[]{:S(2)}) %collective-permute-start.1) | collective-permute-done | bytes 4128 | tf_op jit(solution)/shard_map/ppermute | solution.py:218
  57.7 0.0 copy-start.6
  57.7 0.9 %collective-permute-done.2.s3 = f32[8,128]{1,0:T(8,128)S(1)} collective-permute-done((f32[8,128]{1,0:T(8,128)}, f32[8,128]{1,0:T(8,128)S(1)}, u32[]{:S(2)}, u32[]{:S(2)}) %collective-permute-start.2) | collective-permute-done | bytes 4128 | tf_op jit(solution)/shard_map/ppermute | solution.py:218
  58.6 0.0 copy-start.7
  58.6 0.0 copy-done.2
  58.6 0.0 copy-done.3
  58.6 0.0 copy-done.4
  58.6 0.0 copy-done.5
  58.6 0.0 copy-done.6
  58.6 0.6 copy-done.7
  59.2 2.5 %project.1 = f32[64,256]{1,0:T(8,128)} custom-call(s32[1]{0:T(128)} %bitcast.me, f32[64,8,128]{2,1,0:T(8,128)} %get-tuple-element.18.readout, f32[8,128]{1,0:T(8,128)} %get-tuple-element.13.s0, f32[8,128]{1,0:T(8,128)} %copy-done.5, f32[8,128]{1,0:T(8,128)} %copy-done.6, f32[8,128]{1,0:T(8,128)} %copy-done.7, f32[64,8,128]{2,1,0:T(8,128)} %logits.1, ...), custom_call_target="tpu_custom_call" | custom-call | tf_op jit(solution)/shard_map/project/pallas_call | solution.py:221
  61.6 0.3 collective-permute-start.6
  61.9 1.1 %collective-permute-start.7 = (f32[64,256]{1,0:T(8,128)}, f32[64,256]{1,0:T(8,128)S(1)}, u32[]{:S(2)}, u32[]{:S(2)}) collective-permute-start(f32[64,256]{1,0:T(8,128)} %project.1), channel_id=1, source_target_pairs={{0,2},{1,3},{2,0},{3,1},{4,6},{5,7},{6,4},{7,5},{8,10},{9,11},{10,... | collective-permute-start | bytes 196616 | tf_op jit(solution)/shard_map/ppermute | solution.py:229
  63.1 0.7 %collective-permute-start.8 = (f32[64,256]{1,0:T(8,128)}, f32[64,256]{1,0:T(8,128)S(1)}, u32[]{:S(2)}, u32[]{:S(2)}) collective-permute-start(f32[64,256]{1,0:T(8,128)} %project.1), channel_id=1, source_target_pairs={{0,3},{1,2},{2,1},{3,0},{4,7},{5,6},{6,5},{7,4},{8,11},{9,10},{10,... | collective-permute-start | bytes 196616 | tf_op jit(solution)/shard_map/ppermute | solution.py:229
  63.8 0.0 collective-permute-done.6
  63.8 1.8 %collective-permute-done.7 = f32[64,256]{1,0:T(8,128)S(1)} collective-permute-done((f32[64,256]{1,0:T(8,128)}, f32[64,256]{1,0:T(8,128)S(1)}, u32[]{:S(2)}, u32[]{:S(2)}) %collective-permute-start.7) | collective-permute-done | bytes 65568 | tf_op jit(solution)/shard_map/ppermute | solution.py:229
  65.6 2.0 %collective-permute-done.8 = f32[64,256]{1,0:T(8,128)S(1)} collective-permute-done((f32[64,256]{1,0:T(8,128)}, f32[64,256]{1,0:T(8,128)S(1)}, u32[]{:S(2)}, u32[]{:S(2)}) %collective-permute-start.8) | collective-permute-done | bytes 65568 | tf_op jit(solution)/shard_map/ppermute | solution.py:229
  67.6 1.5 %add_add_fusion = f32[64,256]{1,0:T(8,128)} fusion(f32[64,256]{1,0:T(8,128)S(1)} %collective-permute-done.7, f32[64,256]{1,0:T(8,128)S(1)} %collective-permute-done.8, f32[64,256]{1,0:T(8,128)} %project.1, f32[64,256]{1,0:T(8,128)S(1)} %collective-permute-done.6), kind=kLoop, calls=%fused_computation | loop fusion | flops 49152 | bytes 327680 | tf_op jit(solution)/shard_map/add | solution.py:230
Async XLA Ops:
  0.6 38.4 %copy-start.1 = (bf16[2,128,256]{2,1,0:T(8,128)(2,1)S(1)}, bf16[2,128,256]{2,1,0:T(8,128)(2,1)}, u32[]{:S(2)}) copy-start(bf16[2,128,256]{2,1,0:T(8,128)(2,1)} %w0.1) | copy-start | bytes 393220
  35.5 13.7 %all-to-all-start.1 = ((bf16[16,32,128]{2,1,0:T(8,128)(2,1)}), bf16[16,32,128]{2,1,0:T(8,128)(2,1)S(1)}, u32[]{:S(2)}, u32[]{:S(2)}) async-start(bf16[16,32,128]{2,1,0:T(8,128)(2,1)} %combine.1), calls=%async_computation.1 | async-start | bytes 262144 | tf_op jit(solution)/shard_map/all_to_all | solution.py:214
  39.0 16.3 %collective-permute-start.3 = (bf16[2,128,256]{2,1,0:T(8,128)(2,1)S(1)}, bf16[2,128,256]{2,1,0:T(8,128)(2,1)S(1)}, u32[]{:S(2)}, u32[]{:S(2)}) collective-permute-start(bf16[2,128,256]{2,1,0:T(8,128)(2,1)S(1)} %copy-done.1), channel_id=1, source_target_pairs={{0,64},{64,0},{128,192},{192,128},{1,65},{65,1},{129,193},{193,129... | collective-permute-start | bytes 393224 | tf_op jit(solution)/shard_map/ppermute | solution.py:169
  40.4 16.3 %collective-permute-start.4 = (bf16[2,128,256]{2,1,0:T(8,128)(2,1)S(1)}, bf16[2,128,256]{2,1,0:T(8,128)(2,1)S(1)}, u32[]{:S(2)}, u32[]{:S(2)}) collective-permute-start(bf16[2,128,256]{2,1,0:T(8,128)(2,1)S(1)} %copy-done.1), channel_id=1, source_target_pairs={{0,128},{64,192},{128,0},{192,64},{1,129},{65,193},{129,1},{193,65... | collective-permute-start | bytes 393224 | tf_op jit(solution)/shard_map/ppermute | solution.py:169
  43.0 13.7 %collective-permute-start.5 = (bf16[2,128,256]{2,1,0:T(8,128)(2,1)S(1)}, bf16[2,128,256]{2,1,0:T(8,128)(2,1)S(1)}, u32[]{:S(2)}, u32[]{:S(2)}) collective-permute-start(bf16[2,128,256]{2,1,0:T(8,128)(2,1)S(1)} %copy-done.1), channel_id=1, source_target_pairs={{0,192},{64,128},{128,64},{192,0},{1,193},{65,129},{129,65},{193,1... | collective-permute-start | bytes 393224 | tf_op jit(solution)/shard_map/ppermute | solution.py:169
  49.2 0.6 copy-start
  51.5 5.1 %collective-permute-start = (f32[8,128]{1,0:T(8,128)}, f32[8,128]{1,0:T(8,128)S(1)}, u32[]{:S(2)}, u32[]{:S(2)}) collective-permute-start(f32[8,128]{1,0:T(8,128)} %get-tuple-element.13.s0), channel_id=1, source_target_pairs={{0,1},{1,0},{2,3},{3,2},{4,5},{5,4},{6,7},{7,6},{8,9},{9,8},{10,11... | collective-permute-start | bytes 12296 | tf_op jit(solution)/shard_map/ppermute | solution.py:218
  55.0 2.7 %collective-permute-start.1 = (f32[8,128]{1,0:T(8,128)}, f32[8,128]{1,0:T(8,128)S(1)}, u32[]{:S(2)}, u32[]{:S(2)}) collective-permute-start(f32[8,128]{1,0:T(8,128)} %get-tuple-element.13.s0), channel_id=1, source_target_pairs={{0,2},{1,3},{2,0},{3,1},{4,6},{5,7},{6,4},{7,5},{8,10},{9,11},{10,... | collective-permute-start | bytes 12296 | tf_op jit(solution)/shard_map/ppermute | solution.py:218
  55.3 3.3 %copy-start.2 = (bf16[2,128,256]{2,1,0:T(8,128)(2,1)}, bf16[2,128,256]{2,1,0:T(8,128)(2,1)S(1)}, u32[]{:S(2)}) copy-start(bf16[2,128,256]{2,1,0:T(8,128)(2,1)S(1)} %collective-permute-done.3.w1) | copy-start | bytes 393220
  55.3 3.2 %collective-permute-start.2 = (f32[8,128]{1,0:T(8,128)}, f32[8,128]{1,0:T(8,128)S(1)}, u32[]{:S(2)}, u32[]{:S(2)}) collective-permute-start(f32[8,128]{1,0:T(8,128)} %get-tuple-element.13.s0), channel_id=1, source_target_pairs={{0,3},{1,2},{2,1},{3,0},{4,7},{5,6},{6,5},{7,4},{8,11},{9,10},{10,... | collective-permute-start | bytes 12296 | tf_op jit(solution)/shard_map/ppermute | solution.py:218
  56.7 1.9 %copy-start.3 = (bf16[2,128,256]{2,1,0:T(8,128)(2,1)}, bf16[2,128,256]{2,1,0:T(8,128)(2,1)S(1)}, u32[]{:S(2)}) copy-start(bf16[2,128,256]{2,1,0:T(8,128)(2,1)S(1)} %collective-permute-done.4.w2) | copy-start | bytes 393220
  56.7 1.9 %copy-start.4 = (bf16[2,128,256]{2,1,0:T(8,128)(2,1)}, bf16[2,128,256]{2,1,0:T(8,128)(2,1)S(1)}, u32[]{:S(2)}) copy-start(bf16[2,128,256]{2,1,0:T(8,128)(2,1)S(1)} %collective-permute-done.5.w3) | copy-start | bytes 393220
  56.7 1.9 %copy-start.5 = (f32[8,128]{1,0:T(8,128)}, f32[8,128]{1,0:T(8,128)S(1)}, u32[]{:S(2)}) copy-start(f32[8,128]{1,0:T(8,128)S(1)} %collective-permute-done.s1) | copy-start | bytes 12292
  57.7 0.9 %copy-start.6 = (f32[8,128]{1,0:T(8,128)}, f32[8,128]{1,0:T(8,128)S(1)}, u32[]{:S(2)}) copy-start(f32[8,128]{1,0:T(8,128)S(1)} %collective-permute-done.1.s2) | copy-start | bytes 12292
  58.6 0.6 copy-start.7
  61.6 2.1 %collective-permute-start.6 = (f32[64,256]{1,0:T(8,128)}, f32[64,256]{1,0:T(8,128)S(1)}, u32[]{:S(2)}, u32[]{:S(2)}) collective-permute-start(f32[64,256]{1,0:T(8,128)} %project.1), channel_id=1, source_target_pairs={{0,1},{1,0},{2,3},{3,2},{4,5},{5,4},{6,7},{7,6},{8,9},{9,8},{10,11... | collective-permute-start | bytes 196616 | tf_op jit(solution)/shard_map/ppermute | solution.py:229
  61.9 3.7 %collective-permute-start.7 = (f32[64,256]{1,0:T(8,128)}, f32[64,256]{1,0:T(8,128)S(1)}, u32[]{:S(2)}, u32[]{:S(2)}) collective-permute-start(f32[64,256]{1,0:T(8,128)} %project.1), channel_id=1, source_target_pairs={{0,2},{1,3},{2,0},{3,1},{4,6},{5,7},{6,4},{7,5},{8,10},{9,11},{10,... | collective-permute-start | bytes 196616 | tf_op jit(solution)/shard_map/ppermute | solution.py:229
  63.1 4.5 %collective-permute-start.8 = (f32[64,256]{1,0:T(8,128)}, f32[64,256]{1,0:T(8,128)S(1)}, u32[]{:S(2)}, u32[]{:S(2)}) collective-permute-start(f32[64,256]{1,0:T(8,128)} %project.1), channel_id=1, source_target_pairs={{0,3},{1,2},{2,1},{3,0},{4,7},{5,6},{6,5},{7,4},{8,11},{9,10},{10,... | collective-permute-start | bytes 196616 | tf_op jit(solution)/shard_map/ppermute | solution.py:229

commit v2 on v1

v2 whole, which is shorter than its diff:
```python
import functools

import jax
import jax.numpy as jnp
from jax import lax
from jax.experimental import pallas as pl
from jax.experimental.pallas import tpu as pltpu
from jax.sharding import PartitionSpec as P

H = 8
DK = 256
DV = 512
HB = 4
ROWS = 16
COLS = 4
B = 64
KR = 16
V = 128
OUT = 256
MINE = B // ROWS
BLOCK = 8
NROWS = MINE * H
CHUNK = NROWS + H
NSCALE = 2048.0
DSCALE = 64.0
OSCALE = 64.0
STEP = 256.0
READ_KIB = 65152
WRITE_KIB = 60 * 1024
f32 = jnp.float32
bf16 = jnp.bfloat16
f16 = jnp.float16


def parts_of(x):
    first = x.astype(bf16).astype(f32)
    rest = (x - first) * STEP
    second = rest.astype(bf16).astype(f32)
    third = (rest - second) * STEP
    return first, second, third


def gates(stab, in_gate, forget):
    pre = forget[...]
    log_sig = jnp.minimum(pre, 0.0) - jnp.log(1.0 + jnp.exp(-jnp.abs(pre)))
    carried = log_sig + stab[...]
    fresh = jnp.maximum(carried, in_gate[...])
    return fresh, jnp.exp(carried - fresh), jnp.exp(in_gate[...] - fresh) * DK**-0.5


def over_rows(x, h):
    return jnp.broadcast_to(x[h : h + 1, :], (KR, B))


def fetches(sems, *pairs):
    return [pltpu.make_async_copy(a, b, sems.at[n]) for n, (a, b) in enumerate(pairs)]


def cell_rows(step, count=1):
    return pl.ds(pl.multiple_of(BLOCK * H * KR * step, BLOCK * H * KR), BLOCK * H * KR * count)


def read_kernel(
    cell_h, normal_h, stab_h, query_h, keys_h, value_h, in_gate_h, forget_h,
    new_normal, new_stab, send,
    cell, normal, stab, query, keys, value, in_gate, forget,
    keep_s, mixed_s, high_s, low_s, field_s, sems, cell_sems,
):
    small = fetches(
        sems, (stab_h, stab), (in_gate_h, in_gate), (forget_h, forget), (keys_h, keys),
        (query_h, query), (normal_h, normal), (value_h, value),
    )
    large = [
        pltpu.make_async_copy(cell_h.at[cell_rows(n)], cell.at[cell_rows(n)], cell_sems.at[n])
        for n in range(B // BLOCK)
    ]
    for c in small + large:
        c.start()
    for c in small:
        c.wait()
    read_start(
        normal, stab, query, keys, in_gate, forget, new_normal, new_stab,
        keep_s, mixed_s, high_s, low_s, field_s,
    )

    def body(step, carry):
        pltpu.make_async_copy(
            cell_h.at[cell_rows(step)], cell.at[cell_rows(step)], cell_sems.at[step]
        ).wait()
        read_step(step, cell, value, send, keep_s, mixed_s, high_s, low_s, field_s)
        return carry

    lax.fori_loop(0, B // BLOCK, body, 0)


def read_start(
    normal, stab, query, keys, in_gate, forget, new_normal, new_stab,
    keep_s, mixed_s, high_s, low_s, field_s,
):
    fresh, keep, admit = gates(stab, in_gate, forget)
    new_stab[...] = fresh
    keep_s[:, :B] = keep
    heads = lax.broadcasted_iota(jnp.int32, (H, B), 0)
    denom = jnp.zeros((H, B), f32)
    mixed = jnp.zeros((H, B), f32)
    for h in range(H):
        rows = slice(KR * h, KR * (h + 1))
        add = over_rows(admit, h) * keys[rows, :]
        q = query[rows, :]
        normed = over_rows(keep, h) * normal[rows, :] + add
        new_normal[rows, :] = normed
        denom = jnp.where(heads == h, jnp.sum(q * normed, axis=0, keepdims=True), denom)
        mixed = jnp.where(heads == h, jnp.sum(q * add, axis=0, keepdims=True), mixed)
    mixed_s[:, :B] = mixed
    for n, x in enumerate(parts_of(fresh) + parts_of(denom * DSCALE)):
        field_s[n, :, :B] = x
    q = jnp.transpose(jnp.concatenate([query[...], query[...]], axis=1))[:B, :]
    high = q.astype(bf16).astype(f32)
    high_s[...] = high
    low_s[...] = q - high


def read_step(step, cell, value, send, keep_s, mixed_s, high_s, low_s, field_s):
    back = lax.rem(2 * B - BLOCK * step, 2 * B)
    keep = pltpu.roll(keep_s[...], back, 1)
    mixed = pltpu.roll(mixed_s[...], back, 1)
    heads = lax.broadcasted_iota(jnp.int32, (H, V), 0)
    own = lax.broadcasted_iota(jnp.int32, (H, V), 1) // KR == heads
    for b in range(BLOCK):
        lane = slice(b, b + 1)
        row = pl.ds(BLOCK * step + b, 1)
        high = jnp.where(own, jnp.broadcast_to(high_s[row, :], (H, V)), 0.0)
        low = jnp.where(own, jnp.broadcast_to(low_s[row, :], (H, V)), 0.0)
        q = jnp.concatenate([high, low], axis=0).astype(bf16)
        start = pl.multiple_of((BLOCK * step + b) * H * KR, H * KR)
        held = cell[pl.ds(start, H * KR), :]
        first = held.astype(bf16)
        second = (held - first.astype(f32)).astype(bf16)
        total = jnp.dot(q, first, preferred_element_type=f32)
        total = total + jnp.dot(q, second, preferred_element_type=f32)
        numer = keep[:, lane] * (total[:H] + total[H:]) + mixed[:, lane] * value[BLOCK * step + b]
        at = (BLOCK // MINE) * step + b // MINE
        j = b % MINE
        send[at, H * j : H * (j + 1), :] = numer * NSCALE

    lanes = lax.broadcasted_iota(jnp.int32, (H, 2 * B), 1)
    for c in range(BLOCK // MINE):
        tile = jnp.zeros((H, 2 * B), f32)
        for n in range(6):
            shift = lax.rem(back + (MINE * (n - c)) % (2 * B), 2 * B)
            inside = (lanes >= MINE * n) & (lanes < MINE * (n + 1))
            tile = jnp.where(inside, pltpu.roll(field_s[n], shift, 1), tile)
        send[(BLOCK // MINE) * step + c, NROWS:CHUNK, :] = tile


def halves(x):
    high = x.astype(bf16).astype(f32)
    return jnp.concatenate([high, x - high], axis=1)


def write_kernel(first, steps, cell_h, stab_h, keys_h, value_h, in_gate_h, forget_h, *rest):
    (new_cell_h, cell, new_cell, stab, keys, value, in_gate, forget, factors_s,
     sems, in_sems, out_sems) = rest[-12:]
    seqs = pl.ds(BLOCK * first, BLOCK * steps)
    small = fetches(
        sems, (stab_h, stab), (in_gate_h, in_gate), (forget_h, forget), (keys_h, keys),
        (value_h.at[seqs], value),
    )
    large = [
        pltpu.make_async_copy(cell_h.at[cell_rows(first + n)], cell.at[cell_rows(n)], in_sems.at[n])
        for n in range(steps)
    ]
    for c in small + large:
        c.start()
    for c in small:
        c.wait()
    _, held, admit = gates(stab, in_gate, forget)
    for h in range(H):
        factors_s[KR * h : KR * (h + 1), :] = halves(over_rows(admit, h) * keys[KR * h : KR * (h + 1), :])
        keep = jnp.broadcast_to(held[h : h + 1, :], (8, B))
        factors_s[H * KR + 8 * h : H * KR + 8 * (h + 1), :] = halves(keep)
    factors = factors_s[...].astype(bf16)
    places = lax.rem(lax.broadcasted_iota(jnp.int32, (2 * B, V), 0), B)

    def body(n, carry):
        pltpu.make_async_copy(
            cell_h.at[cell_rows(first + n)], cell.at[cell_rows(n)], in_sems.at[n]
        ).wait()
        for b in range(BLOCK):
            seq = BLOCK * n + b
            pick = jnp.where(places == BLOCK * first + seq, 1.0, 0.0).astype(bf16)
            spread = jnp.dot(factors, pick, preferred_element_type=f32)
            for h in range(H):
                keep = spread[H * KR + 8 * h : H * KR + 8 * (h + 1), :]
                v = value[seq, h : h + 1, :]
                for t in range(KR * h, KR * (h + 1), 8):
                    rows = pl.ds(pl.multiple_of(seq * H * KR + t, 8), 8)
                    new_cell[rows, :] = keep * cell[rows, :] + spread[t : t + 8, :] * v
        pltpu.make_async_copy(
            new_cell.at[cell_rows(n)], new_cell_h.at[cell_rows(first + n)], out_sems.at[n]
        ).start()
        return carry

    lax.fori_loop(0, steps, body, 0)
    for n in range(steps):
        pltpu.make_async_copy(
            new_cell.at[cell_rows(n)], new_cell_h.at[cell_rows(first + n)], out_sems.at[n]
        ).wait()


def combine_kernel(got, out):
    def field(tile, n):
        back = lambda k: pltpu.roll(tile, (-MINE * k) % V, 1) if k else tile
        return back(n) + (back(n + 1) + back(n + 2) * (1.0 / STEP)) * (1.0 / STEP)

    tiles = [got[r, NROWS:CHUNK, :] for r in range(ROWS)]
    stabs = [field(t, 0) for t in tiles]
    top = stabs[0]
    for s in stabs[1:]:
        top = jnp.maximum(top, s)
    scales = [jnp.exp(s - top) for s in stabs]
    denom = scales[0] * field(tiles[0], 3)
    for s, t in zip(scales[1:], tiles[1:]):
        denom = denom + s * field(t, 3)
    base = jnp.maximum(jnp.abs(denom * (1.0 / DSCALE)), jnp.exp(-top)) * NSCALE
    for j in range(MINE):
        lane = slice(j, j + 1)
        rows = slice(H * j, H * (j + 1))
        numer = scales[0][:, lane] * got[0, rows, :]
        for r in range(1, ROWS):
            numer = numer + scales[r][:, lane] * got[r, rows, :]
        readout = (numer / jnp.broadcast_to(base[:, lane], (H, V))).astype(bf16)
        for r in range(ROWS):
            out[r, rows, :] = readout


def stats_kernel(got, readout, stats):
    lanes = lax.broadcasted_iota(jnp.int32, (H, 2 * B), 1)
    tile = jnp.zeros((H, 2 * B), f32)
    for b in range(B):
        x = got[b * H : (b + 1) * H, :].astype(f32)
        readout[b] = x
        total = jnp.sum(x, axis=1, keepdims=True)
        square = jnp.sum(x * x, axis=1, keepdims=True)
        tile = jnp.where(lanes == b, total, tile)
        tile = jnp.where(lanes == B + b, square, tile)
    stats[...] = tile


def gate_kernel(logits, gain, weight, out, weight_out):
    g = gain[...]
    for b in range(B):
        out[b] = g / (1.0 + jnp.exp(-logits[b]))
    weight_out[...] = weight[...]


def project_kernel(me, got, stats, gate, w0, w1, w2, w3, out, gated):
    total = ((stats[0] + stats[1]) + (stats[2] + stats[3])) * (1.0 / DV)
    square = pltpu.roll(total, B, 1)
    scale = lax.rsqrt(square - total * total + 1e-06)
    for b in range(B):
        lane = slice(b, b + 1)
        rows = slice(b * H, (b + 1) * H)
        gated[rows, :] = (got[rows, :].astype(f32) - total[:, lane]) * (scale[:, lane] * gate[b])
    acc = jnp.zeros((B, OUT), f32)
    for k, w in enumerate((w0, w1, w2, w3)):
        for j in range(H // HB):
            head = 2 * (me[0] ^ k) + j
            x = gated[pl.ds(head, B, stride=H), :]
            high = x.astype(bf16)
            low = (x - high.astype(f32)).astype(bf16)
            acc = acc + jnp.dot(high, w[j], preferred_element_type=f32)
            acc = acc + jnp.dot(low, w[j], preferred_element_type=f32)
    out[...] = acc * OSCALE


def xor_pairs(n, k):
    return [(i, i ^ k) for i in range(n)]


def local(
    cell_state,
    normalizer,
    stabilizer,
    queries,
    key_vectors,
    token_value_vectors,
    input_gate,
    forget_gate,
    output_gate_logits,
    norm_gain,
    out_weight,
):
    shape = jax.ShapeDtypeStruct
    vmem = pl.BlockSpec(memory_space=pltpu.VMEM)
    weights = [out_weight]
    for k in (1, 2, 3):
        weights.append(lax.ppermute(out_weight, "hb", xor_pairs(HB, k)))
    turned = lambda x: jnp.transpose(x, (1, 2, 0)).reshape(H * KR, B)
    cells = cell_state.reshape(B * H * KR, V)
    stab = jnp.transpose(stabilizer[:, :, 0])
    keys = turned(key_vectors)
    in_gate = jnp.transpose(input_gate)
    forget = jnp.transpose(forget_gate)
    anywhere = pl.BlockSpec(memory_space=pl.ANY)
    rows_s = pltpu.VMEM((H * KR, B), f32)
    gate_s = pltpu.VMEM((H, B), f32)
    new_normal, new_stab, send = pl.pallas_call(
        read_kernel,
        in_specs=[anywhere] * 8,
        out_specs=[vmem] * 3,
        out_shape=[
            shape((H * KR, B), f32),
            shape((H, B), f32),
            shape((ROWS, CHUNK, V), f32),
        ],
        scratch_shapes=[
            pltpu.VMEM((B * H * KR, V), f32),
            rows_s,
            gate_s,
            rows_s,
            rows_s,
            pltpu.VMEM((B, H, V), f32),
            gate_s,
            gate_s,
            pltpu.VMEM((H, 2 * B), f32),
            pltpu.VMEM((H, 2 * B), f32),
            pltpu.VMEM((B, V), f32),
            pltpu.VMEM((B, V), f32),
            pltpu.VMEM((6, H, 2 * B), f32),
            pltpu.SemaphoreType.DMA((7,)),
            pltpu.SemaphoreType.DMA((B // BLOCK,)),
        ],
        name="read",
        compiler_params=pltpu.CompilerParams(vmem_limit_bytes=READ_KIB << 10),
    )(cells, turned(normalizer), stab, turned(queries), keys, token_value_vectors, in_gate, forget)

    def written(first, steps, *before):
        size = BLOCK * steps
        return pl.pallas_call(
            functools.partial(write_kernel, first, steps),
            in_specs=[anywhere] * (6 + len(before)),
            out_specs=anywhere,
            out_shape=shape((B * H * KR, V), f32),
            scratch_shapes=[
                pltpu.VMEM((size * H * KR, V), f32),
                pltpu.VMEM((size * H * KR, V), f32),
                gate_s,
                rows_s,
                pltpu.VMEM((size, H, V), f32),
                gate_s,
                gate_s,
                pltpu.VMEM((H * KR + 8 * H, 2 * B), f32),
                pltpu.SemaphoreType.DMA((5,)),
                pltpu.SemaphoreType.DMA((steps,)),
                pltpu.SemaphoreType.DMA((steps,)),
            ],
            input_output_aliases={6: 0} if before else {},
            compiler_params=pltpu.CompilerParams(vmem_limit_bytes=WRITE_KIB << 10),
            cost_estimate=pl.CostEstimate(flops=0, bytes_accessed=steps << 20, transcendentals=0),
        )(cells, stab, keys, token_value_vectors, in_gate, forget, *before)

    half = B // BLOCK // 2
    new_cell = written(0, half)
    new_cell = written(half, half, new_cell)
    send = send.astype(f16)
    got = lax.all_to_all(send, "row", 0, 0, tiled=True)
    got = got.astype(f32)
    mine = pl.pallas_call(
        combine_kernel,
        in_specs=[vmem],
        out_specs=vmem,
        out_shape=shape((ROWS, NROWS, V), bf16),
        name="combine",
        compiler_params=pltpu.CompilerParams(vmem_limit_bytes=4 << 20),
    )(got)
    every = lax.all_to_all(mine, "row", 0, 0, tiled=True)
    every = every.reshape(B * H, V)
    gate, weights[0] = pl.pallas_call(
        gate_kernel,
        in_specs=[vmem] * 3,
        out_specs=[vmem] * 2,
        out_shape=[shape((B, H, V), f32), shape(out_weight.shape, bf16)],
        name="gate",
        compiler_params=pltpu.CompilerParams(vmem_limit_bytes=4 << 20),
    )(output_gate_logits, norm_gain, out_weight)
    readout, stats = pl.pallas_call(
        stats_kernel,
        in_specs=[vmem],
        out_specs=[vmem] * 2,
        out_shape=[shape((B, H, V), f32), shape((H, 2 * B), f32)],
        name="stats",
        compiler_params=pltpu.CompilerParams(vmem_limit_bytes=4 << 20),
    )(every)
    stats = lax.all_gather(stats, "col")
    me = lax.axis_index("hb").astype(jnp.int32).reshape(1)
    partial_value = pl.pallas_call(
        project_kernel,
        in_specs=[pl.BlockSpec(memory_space=pltpu.SMEM)] + [vmem] * 7,
        out_specs=vmem,
        out_shape=shape((B, OUT), f32),
        scratch_shapes=[pltpu.VMEM((B * H, V), f32)],
        name="project",
        compiler_params=pltpu.CompilerParams(vmem_limit_bytes=6 << 20),
    )(me, every, stats, gate, *weights)
    sent = [lax.optimization_barrier(partial_value.astype(f16))]
    for k in range(1, COLS):
        sent.append(lax.ppermute(sent[0], "col", xor_pairs(COLS, k)))
    sent = [x.astype(f32) for x in sent]
    layer_out = ((sent[0] + sent[1]) + (sent[2] + sent[3])) * (1.0 / OSCALE)
    return (
        layer_out,
        readout,
        new_cell.reshape(B, H, KR, V),
        jnp.transpose(new_normal.reshape(H, KR, B), (2, 0, 1)),
        jnp.transpose(new_stab)[:, :, None],
    )


def solution(mesh):
    in_specs = (
        P("hb", None, "row", "col"),
        P("hb", None, "row"),
        P("hb", None, "row"),
        P("hb", None, "row"),
        P("hb", None, "row"),
        P("hb", None, "col"),
        P("hb", None),
        P("hb", None),
        P("hb", None, "col"),
        P(None, "col"),
        P("hb", "col", "row"),
    )
    out_specs = (
        P("hb", "row"),
        P("hb", None, "col"),
        P("hb", None, "row", "col"),
        P("hb", None, "row"),
        P("hb", None, "row"),
    )
    return jax.shard_map(local, mesh=mesh, in_specs=in_specs, out_specs=out_specs, check_vma=False)
```

time: 69.6 us -> 63.5 us (0.912)
  blocking collectives: 21.6 us -> 30.1 us
  waiting for transfers between devices: 11.9 us -> 5.17 us
  starting transfers between devices: 14.8 us -> 9.75 us
  other arithmetic: 3.24 us -> 1.68 us
  Pallas kernels: 15.6 us -> 14.8 us
    all_gather x0 -> x1, blocking collectives: none -> 8.5 us  [local(): stats = lax.all_gather(stats, 'col')]
    ppermute x9 -> x6, waiting for transfers between devices: 5.71 us -> 0.02 us  [the longest x3 0.01 us: local(): weights.append(lax.ppermute(out_weight, 'hb', xor_pairs(HB, k)))]
    ppermute x9 -> x6, starting transfers between devices: 11.3 us -> 6.23 us  [the longest x3 4.01 us: local(): weights.append(lax.ppermute(out_weight, 'hb', xor_pairs(HB, k)))]
    pallas_call x1, Pallas kernels: 2.47 us -> 0.61 us  [local(): pl.pallas_call(project_kernel, in_specs=[pl.BlockSpec(memory_space=pltpu....]
    add x1 -> x0, other arithmetic: 1.49 us -> none  [local(): layer_out = partial_value + sent[0] + (sent[1] + sent[2])]
    pallas_call x3 -> x6, Pallas kernels: 13.1 us -> 14.2 us  [the longest x2 7.1 us: written(): pl.pallas_call(functools.partial(write_kernel, first, steps), in_specs=[a...]
    all_to_all x1, waiting for transfers between devices: 6.16 us -> 5.15 us  [local(): every = lax.all_to_all(mine, 'row', 0, 0, tiled=True)]
    convert_element_type x2 -> x3, other arithmetic: 1.75 us -> 1.03 us  [the longest x1 1 us: local(): send = send.astype(f16)]
  transfers between devices with their start and end apart: 10 -> 7, of which waited for: 5 -> 1; matrix products, arithmetic and copies ran while one was open for 0% -> 0% of each run, Pallas kernels for 2% -> 13%
where the time goes in v2:
time: 63.5 us; the launch traced here: 63.2 us
  blocking collectives  30.1 us (47%)
  Pallas kernels  14.8 us (23%)
  starting transfers between devices  9.75 us (15%)
  waiting for transfers between devices  5.17 us (8%)
  other arithmetic  1.68 us (3%)
  local copies, waits for them, and re-layouts  0.94 us (1%)
  between operations  0.74 us (1%)
    all_to_all x1, blocking collectives, local(): got = lax.all_to_all(send, 'row', 0, 0, tiled=True)  21.6 us
    all_gather x1, blocking collectives, local(): stats = lax.all_gather(stats, 'col')  8.5 us
    pallas_call x2, Pallas kernels, written(): pl.pallas_call(functools.partial(write_kernel, first, steps), in_specs=[a...  7.1 us
    pallas_call x1, Pallas kernels, local(): pl.pallas_call(read_kernel, in_specs=[anywhere] * 8, out_specs=[vmem] * 3...  5.32 us
    all_to_all x1, waiting for transfers between devices, local(): every = lax.all_to_all(mine, 'row', 0, 0, tiled=True)  5.15 us
    ppermute x3, starting transfers between devices, local(): weights.append(lax.ppermute(out_weight, 'hb', xor_pairs(HB, k)))  4.01 us
    all_to_all x1, starting transfers between devices, local(): every = lax.all_to_all(mine, 'row', 0, 0, tiled=True)  3.51 us
    ppermute x3, starting transfers between devices, local(): sent.append(lax.ppermute(sent[0], 'col', xor_pairs(COLS, k)))  2.23 us
  transfers between devices with their start and end apart: 7, of which 1 were waited for; matrix products, arithmetic and copies ran while one was open for 0% of the time, Pallas kernels for 13%

profile of v2, /device:TPU:1, one launch (start us, length us, event | category | flops | bytes accessed | tf_op | source)
XLA Modules:
  0.0 63.2 jit_solution(12968172851021032507)
XLA Ops:
  0.6 0.0 copy-start.2
  0.6 0.0 copy-start
  0.7 5.3 %read.1 = (f32[128,64]{1,0:T(8,128)}, f32[8,64]{1,0:T(8,128)}, f32[16,40,128]{2,1,0:T(8,128)}) custom-call(f32[8192,128]{1,0:T(8,128)} %bitcast.30, f32[128,64]{1,0:T(8,128)} %bitcast.37, f32[8,64]{1,0:T(8,128)} %bitcast.39, f32[128,64]{1,0:T(8,128)} %bitcast.38, f32[128,64]{1,0:T(8,128)} %bitcast.34, f32[64,8,128]{2,1,0:T(8,128)} %value_h.5, ...), custom_call_target="tpu_custom_call" | custom-call | tf_op jit(solution)/shard_map/read/pallas_call | solution.py:308
  6.0 1.0 %convert_element_type.21 = f16[16,40,128]{2,1,0:T(8,128)(2,1)S(1)} convert(f32[16,40,128]{2,1,0:T(8,128)} %get-tuple-element.12) | non-fusion elementwise | flops 81920 | bytes 491520 | tf_op jit(solution)/shard_map/convert_element_type | solution.py:366
  7.0 21.6 %all_to_all.10 = f16[16,40,128]{2,1,0:T(8,128)(2,1)S(1)} all-to-all(f16[16,40,128]{2,1,0:T(8,128)(2,1)S(1)} %convert_element_type.21), channel_id=1, replica_groups=mesh['hb'=4,'row'=16,'col'=4] {'row'}, dimensions={0} | all-to-all | bytes 327680 | tf_op jit(solution)/shard_map/all_to_all | solution.py:367
  28.6 0.9 %combine.1 = bf16[16,32,128]{2,1,0:T(8,128)(2,1)} custom-call(f32[16,40,128]{2,1,0:T(8,128)S(1)} %convert_element_type.22.got), custom_call_target="tpu_custom_call" | custom-call | tf_op jit(solution)/shard_map/combine/pallas_call | solution.py:369
  29.6 3.5 %all-to-all-start.1 = ((bf16[16,32,128]{2,1,0:T(8,128)(2,1)}), bf16[16,32,128]{2,1,0:T(8,128)(2,1)S(1)}, u32[]{:S(2)}, u32[]{:S(2)}) async-start(bf16[16,32,128]{2,1,0:T(8,128)(2,1)} %combine.1), calls=%async_computation.1 | async-start | bytes 262144 | tf_op jit(solution)/shard_map/all_to_all | solution.py:377
  33.1 1.4 %collective-permute-start = (bf16[2,128,256]{2,1,0:T(8,128)(2,1)}, bf16[2,128,256]{2,1,0:T(8,128)(2,1)S(1)}, u32[]{:S(2)}, u32[]{:S(2)}) collective-permute-start(bf16[2,128,256]{2,1,0:T(8,128)(2,1)} %weight.1), channel_id=1, source_target_pairs={{0,64},{64,0},{128,192},{192,128},{1,65},{65,1},{129,193},{193,129... | collective-permute-start | bytes 393224 | tf_op jit(solution)/shard_map/ppermute | solution.py:298
  34.5 1.9 %collective-permute-start.2 = (bf16[2,128,256]{2,1,0:T(8,128)(2,1)}, bf16[2,128,256]{2,1,0:T(8,128)(2,1)S(1)}, u32[]{:S(2)}, u32[]{:S(2)}) collective-permute-start(bf16[2,128,256]{2,1,0:T(8,128)(2,1)} %weight.1), channel_id=1, source_target_pairs={{0,192},{64,128},{128,64},{192,0},{1,193},{65,129},{129,65},{193,1... | collective-permute-start | bytes 393224 | tf_op jit(solution)/shard_map/ppermute | solution.py:298
  36.4 0.7 %collective-permute-start.1 = (bf16[2,128,256]{2,1,0:T(8,128)(2,1)}, bf16[2,128,256]{2,1,0:T(8,128)(2,1)S(1)}, u32[]{:S(2)}, u32[]{:S(2)}) collective-permute-start(bf16[2,128,256]{2,1,0:T(8,128)(2,1)} %weight.1), channel_id=1, source_target_pairs={{0,128},{64,192},{128,0},{192,64},{1,129},{65,193},{129,1},{193,65... | collective-permute-start | bytes 393224 | tf_op jit(solution)/shard_map/ppermute | solution.py:298
  37.1 0.0 copy-done.2
  37.1 0.0 copy-done
  37.1 0.0 copy-start.1
  37.1 0.9 %copy-done.1 = bf16[2,128,256]{2,1,0:T(8,128)(2,1)S(1)} copy-done((bf16[2,128,256]{2,1,0:T(8,128)(2,1)S(1)}, bf16[2,128,256]{2,1,0:T(8,128)(2,1)}, u32[]{:S(2)}) %copy-start.1) | copy-done | bytes 131096
  38.1 0.1 gate.1
  38.1 5.2 %all-to-all-done.1 = bf16[16,32,128]{2,1,0:T(8,128)(2,1)S(1)} async-done(((bf16[16,32,128]{2,1,0:T(8,128)(2,1)}), bf16[16,32,128]{2,1,0:T(8,128)(2,1)S(1)}, u32[]{:S(2)}, u32[]{:S(2)}) %all-to-all-start.1) | async-done | bytes 131104 | tf_op jit(solution)/shard_map/all_to_all | solution.py:377
  43.3 0.7 %stats.1 = (f32[64,8,128]{2,1,0:T(8,128)}, f32[8,128]{1,0:T(8,128)S(1)}) custom-call(bf16[512,128]{1,0:T(8,128)(2,1)S(1)} %bitcast.27), custom_call_target="tpu_custom_call" | custom-call | tf_op jit(solution)/shard_map/stats/pallas_call | solution.py:387
  44.0 8.5 %all-gather = f32[32,128]{1,0:T(8,128)S(1)} all-gather(f32[8,128]{1,0:T(8,128)S(1)} %get-tuple-element.13), channel_id=2, replica_groups=mesh['hb'=4,'row'=16,'col'=4] {'col'}, dimensions={0}, use_global_device_ids=true | all-gather | bytes 20480 | tf_op jit(solution)/shard_map/all_gather | solution.py:395
  52.5 0.0 collective-permute-done.w1
  52.5 0.0 collective-permute-done.2.w3
  52.5 0.0 collective-permute-done.1.w2
  52.5 0.6 project.1
  53.2 0.4 collective-permute-start.5
  53.6 1.2 %collective-permute-start.4 = (f16[64,256]{1,0:T(8,128)(2,1)S(1)}, f16[64,256]{1,0:T(8,128)(2,1)S(1)}, u32[]{:S(2)}, u32[]{:S(2)}) collective-permute-start(f16[64,256]{1,0:T(8,128)(2,1)S(1)} %convert_element_type.23), channel_id=1, source_target_pairs={{0,2},{1,3},{2,0},{3,1},{4,6},{5,7},{6,4},{7,5},{8,10},{9,11},{10,... | collective-permute-start | bytes 98312 | tf_op jit(solution)/shard_map/ppermute | solution.py:408
  54.8 0.6 collective-permute-start.3
  55.4 3.5 %shard_map.146.rest_0_ = f32[8192,128]{1,0:T(8,128)} custom-call(f32[8192,128]{1,0:T(8,128)} %bitcast.31, f32[8,64]{1,0:T(8,128)} %bitcast.40, f32[128,64]{1,0:T(8,128)} %bitcast.35, f32[64,8,128]{2,1,0:T(8,128)} %value_h.5, f32[8,64]{1,0:T(8,128)} %bitcast.43, f32[8,64]{1,0:T(8,128)} %bitcast.46), custom_call_target="tpu_custom_call" | custom-call | bytes 4194304 | tf_op jit(solution)/shard_map/pallas_call | solution.py:340
  59.0 3.6 %shard_map.147 = f32[8192,128]{1,0:T(8,128)} custom-call(f32[8192,128]{1,0:T(8,128)} %bitcast.32, f32[8,64]{1,0:T(8,128)} %bitcast.41, f32[128,64]{1,0:T(8,128)} %bitcast.36, f32[64,8,128]{2,1,0:T(8,128)} %value_h.5, f32[8,64]{1,0:T(8,128)} %bitcast.44, f32[8,64]{1,0:T(8,128)} %bitcast.47, ...), custom_call_target="tpu_custom_call", output_to_operand_aliasing={{}: (6, {})} | custom-call | bytes 4194304 | tf_op jit(solution)/shard_map/pallas_call | solution.py:340
  62.5 0.0 collective-permute-done.5
  62.5 0.0 collective-permute-done.4
  62.5 0.0 collective-permute-done.3
  62.5 0.7 %add_multiply_fusion = f32[64,256]{1,0:T(8,128)} fusion(f16[64,256]{1,0:T(8,128)(2,1)S(1)} %collective-permute-done.5, f16[64,256]{1,0:T(8,128)(2,1)S(1)} %collective-permute-done.4, f16[64,256]{1,0:T(8,128)(2,1)S(1)} %collective-permute-done.3, f16[64,256]{1,0:T(8,128)(2,1)S(1)} %convert_element_type.23), kind=kLoop, calls=%fused_computation | loop fusion | flops 131072 | bytes 196608 | tf_op jit(solution)/shard_map/mul | solution.py:410
  (2 shorter events, 0.0 us)
Async XLA Ops:
  0.6 36.5 %copy-start.2 = (f32[8,128]{1,0:T(8,128)S(1)}, f32[8,128]{1,0:T(8,128)}, u32[]{:S(2)}) copy-start(f32[8,128]{1,0:T(8,128)} %gain.1) | copy-start | bytes 12292
  0.6 36.5 %copy-start = (f32[64,8,128]{2,1,0:T(8,128)S(1)}, f32[64,8,128]{2,1,0:T(8,128)}, u32[]{:S(2)}) copy-start(f32[64,8,128]{2,1,0:T(8,128)} %logits.1) | copy-start | bytes 786436
  29.6 13.7 %all-to-all-start.1 = ((bf16[16,32,128]{2,1,0:T(8,128)(2,1)}), bf16[16,32,128]{2,1,0:T(8,128)(2,1)S(1)}, u32[]{:S(2)}, u32[]{:S(2)}) async-start(bf16[16,32,128]{2,1,0:T(8,128)(2,1)} %combine.1), calls=%async_computation.1 | async-start | bytes 262144 | tf_op jit(solution)/shard_map/all_to_all | solution.py:377
  33.1 19.4 %collective-permute-start = (bf16[2,128,256]{2,1,0:T(8,128)(2,1)}, bf16[2,128,256]{2,1,0:T(8,128)(2,1)S(1)}, u32[]{:S(2)}, u32[]{:S(2)}) collective-permute-start(bf16[2,128,256]{2,1,0:T(8,128)(2,1)} %weight.1), channel_id=1, source_target_pairs={{0,64},{64,0},{128,192},{192,128},{1,65},{65,1},{129,193},{193,129... | collective-permute-start | bytes 393224 | tf_op jit(solution)/shard_map/ppermute | solution.py:298
  34.5 18.0 %collective-permute-start.2 = (bf16[2,128,256]{2,1,0:T(8,128)(2,1)}, bf16[2,128,256]{2,1,0:T(8,128)(2,1)S(1)}, u32[]{:S(2)}, u32[]{:S(2)}) collective-permute-start(bf16[2,128,256]{2,1,0:T(8,128)(2,1)} %weight.1), channel_id=1, source_target_pairs={{0,192},{64,128},{128,64},{192,0},{1,193},{65,129},{129,65},{193,1... | collective-permute-start | bytes 393224 | tf_op jit(solution)/shard_map/ppermute | solution.py:298
  36.4 16.1 %collective-permute-start.1 = (bf16[2,128,256]{2,1,0:T(8,128)(2,1)}, bf16[2,128,256]{2,1,0:T(8,128)(2,1)S(1)}, u32[]{:S(2)}, u32[]{:S(2)}) collective-permute-start(bf16[2,128,256]{2,1,0:T(8,128)(2,1)} %weight.1), channel_id=1, source_target_pairs={{0,128},{64,192},{128,0},{192,64},{1,129},{65,193},{129,1},{193,65... | collective-permute-start | bytes 393224 | tf_op jit(solution)/shard_map/ppermute | solution.py:298
  37.1 0.9 %copy-start.1 = (bf16[2,128,256]{2,1,0:T(8,128)(2,1)S(1)}, bf16[2,128,256]{2,1,0:T(8,128)(2,1)}, u32[]{:S(2)}) copy-start(bf16[2,128,256]{2,1,0:T(8,128)(2,1)} %weight.1) | copy-start | bytes 393220
  53.2 9.3 %collective-permute-start.5 = (f16[64,256]{1,0:T(8,128)(2,1)S(1)}, f16[64,256]{1,0:T(8,128)(2,1)S(1)}, u32[]{:S(2)}, u32[]{:S(2)}) collective-permute-start(f16[64,256]{1,0:T(8,128)(2,1)S(1)} %convert_element_type.23), channel_id=1, source_target_pairs={{0,3},{1,2},{2,1},{3,0},{4,7},{5,6},{6,5},{7,4},{8,11},{9,10},{10,... | collective-permute-start | bytes 98312 | tf_op jit(solution)/shard_map/ppermute | solution.py:408
  53.6 8.9 %collective-permute-start.4 = (f16[64,256]{1,0:T(8,128)(2,1)S(1)}, f16[64,256]{1,0:T(8,128)(2,1)S(1)}, u32[]{:S(2)}, u32[]{:S(2)}) collective-permute-start(f16[64,256]{1,0:T(8,128)(2,1)S(1)} %convert_element_type.23), channel_id=1, source_target_pairs={{0,2},{1,3},{2,0},{3,1},{4,6},{5,7},{6,4},{7,5},{8,10},{9,11},{10,... | collective-permute-start | bytes 98312 | tf_op jit(solution)/shard_map/ppermute | solution.py:408
  54.8 7.8 %collective-permute-start.3 = (f16[64,256]{1,0:T(8,128)(2,1)S(1)}, f16[64,256]{1,0:T(8,128)(2,1)S(1)}, u32[]{:S(2)}, u32[]{:S(2)}) collective-permute-start(f16[64,256]{1,0:T(8,128)(2,1)S(1)} %convert_element_type.23), channel_id=1, source_target_pairs={{0,1},{1,0},{2,3},{3,2},{4,5},{5,4},{6,7},{7,6},{8,9},{9,8},{10,11... | collective-permute-start | bytes 98312 | tf_op jit(solution)/shard_map/ppermute | solution.py:408

commit v3 on v2

--- a/solution.py
+++ b/solution.py
@@ -64,7 +64,7 @@
     cell_h, normal_h, stab_h, query_h, keys_h, value_h, in_gate_h, forget_h,
     new_normal, new_stab, send,
     cell, normal, stab, query, keys, value, in_gate, forget,
-    keep_s, mixed_s, high_s, low_s, field_s, sems, cell_sems,
+    keep_s, mixed_s, high_s, low_s, sems, cell_sems,
 ):
     small = fetches(
         sems, (stab_h, stab), (in_gate_h, in_gate), (forget_h, forget), (keys_h, keys),
@@ -79,23 +79,23 @@
     for c in small:
         c.wait()
     read_start(
-        normal, stab, query, keys, in_gate, forget, new_normal, new_stab,
-        keep_s, mixed_s, high_s, low_s, field_s,
+        normal, stab, query, keys, in_gate, forget, new_normal, new_stab, send,
+        keep_s, mixed_s, high_s, low_s,
     )
 
     def body(step, carry):
         pltpu.make_async_copy(
             cell_h.at[cell_rows(step)], cell.at[cell_rows(step)], cell_sems.at[step]
         ).wait()
-        read_step(step, cell, value, send, keep_s, mixed_s, high_s, low_s, field_s)
+        read_step(step, cell, value, send, keep_s, mixed_s, high_s, low_s)
         return carry
 
     lax.fori_loop(0, B // BLOCK, body, 0)
 
 
 def read_start(
-    normal, stab, query, keys, in_gate, forget, new_normal, new_stab,
-    keep_s, mixed_s, high_s, low_s, field_s,
+    normal, stab, query, keys, in_gate, forget, new_normal, new_stab, send,
+    keep_s, mixed_s, high_s, low_s,
 ):
     fresh, keep, admit = gates(stab, in_gate, forget)
     new_stab[...] = fresh
@@ -112,15 +112,25 @@
         denom = jnp.where(heads == h, jnp.sum(q * normed, axis=0, keepdims=True), denom)
         mixed = jnp.where(heads == h, jnp.sum(q * add, axis=0, keepdims=True), mixed)
     mixed_s[:, :B] = mixed
-    for n, x in enumerate(parts_of(fresh) + parts_of(denom * DSCALE)):
-        field_s[n, :, :B] = x
+    fields = parts_of(fresh) + parts_of(denom * DSCALE)
+    count = len(fields)
+    groups = lax.broadcasted_iota(jnp.int32, (H, 2 * B), 1) // MINE
+    wide = [jnp.concatenate([x, jnp.zeros_like(x)], axis=1) for x in fields]
+    wide = [pltpu.roll(x, MINE * n, 1) if n else x for n, x in enumerate(wide)]
+    for first in range(count):
+        packed = wide[0]
+        for n in range(1, count):
+            packed = jnp.where(lax.rem(groups + (count - first), count) == n, wide[n], packed)
+        for r in range(first, ROWS, count):
+            tile = pltpu.roll(packed, 2 * B - MINE * r, 1) if r else packed
+            send[r, NROWS:CHUNK, :] = tile
     q = jnp.transpose(jnp.concatenate([query[...], query[...]], axis=1))[:B, :]
     high = q.astype(bf16).astype(f32)
     high_s[...] = high
     low_s[...] = q - high
 
 
-def read_step(step, cell, value, send, keep_s, mixed_s, high_s, low_s, field_s):
+def read_step(step, cell, value, send, keep_s, mixed_s, high_s, low_s):
     back = lax.rem(2 * B - BLOCK * step, 2 * B)
     keep = pltpu.roll(keep_s[...], back, 1)
     mixed = pltpu.roll(mixed_s[...], back, 1)
@@ -143,15 +153,6 @@
         j = b % MINE
         send[at, H * j : H * (j + 1), :] = numer * NSCALE
 
-    lanes = lax.broadcasted_iota(jnp.int32, (H, 2 * B), 1)
-    for c in range(BLOCK // MINE):
-        tile = jnp.zeros((H, 2 * B), f32)
-        for n in range(6):
-            shift = lax.rem(back + (MINE * (n - c)) % (2 * B), 2 * B)
-            inside = (lanes >= MINE * n) & (lanes < MINE * (n + 1))
-            tile = jnp.where(inside, pltpu.roll(field_s[n], shift, 1), tile)
-        send[(BLOCK // MINE) * step + c, NROWS:CHUNK, :] = tile
-
 
 def halves(x):
     high = x.astype(bf16).astype(f32)
@@ -254,8 +255,8 @@
     weight_out[...] = weight[...]
 
 
-def project_kernel(me, got, stats, gate, w0, w1, w2, w3, out, gated):
-    total = ((stats[0] + stats[1]) + (stats[2] + stats[3])) * (1.0 / DV)
+def project_kernel(me, got, s0, s1, s2, s3, gate, w0, w1, w2, w3, out, gated):
+    total = ((s0[...] + s1[...]) + (s2[...] + s3[...])) * (1.0 / DV)
     square = pltpu.roll(total, B, 1)
     scale = lax.rsqrt(square - total * total + 1e-06)
     for b in range(B):
@@ -327,7 +328,6 @@
             pltpu.VMEM((H, 2 * B), f32),
             pltpu.VMEM((B, V), f32),
             pltpu.VMEM((B, V), f32),
-            pltpu.VMEM((6, H, 2 * B), f32),
             pltpu.SemaphoreType.DMA((7,)),
             pltpu.SemaphoreType.DMA((B // BLOCK,)),
         ],
@@ -361,8 +361,8 @@
         )(cells, stab, keys, token_value_vectors, in_gate, forget, *before)
 
     half = B // BLOCK // 2
-    new_cell = written(0, half)
-    new_cell = written(half, half, new_cell)
+    new_cell = written(0, half + half // 2)
+    new_cell = written(half + half // 2, half // 2, new_cell)
     send = send.astype(f16)
     got = lax.all_to_all(send, "row", 0, 0, tiled=True)
     got = got.astype(f32)
@@ -392,17 +392,19 @@
         name="stats",
         compiler_params=pltpu.CompilerParams(vmem_limit_bytes=4 << 20),
     )(every)
-    stats = lax.all_gather(stats, "col")
+    stats = [stats]
+    for k in range(1, COLS):
+        stats.append(lax.ppermute(stats[0], "col", xor_pairs(COLS, k)))
     me = lax.axis_index("hb").astype(jnp.int32).reshape(1)
     partial_value = pl.pallas_call(
         project_kernel,
-        in_specs=[pl.BlockSpec(memory_space=pltpu.SMEM)] + [vmem] * 7,
+        in_specs=[pl.BlockSpec(memory_space=pltpu.SMEM)] + [vmem] * 10,
         out_specs=vmem,
         out_shape=shape((B, OUT), f32),
         scratch_shapes=[pltpu.VMEM((B * H, V), f32)],
         name="project",
         compiler_params=pltpu.CompilerParams(vmem_limit_bytes=6 << 20),
-    )(me, every, stats, gate, *weights)
+    )(me, every, *stats, gate, *weights)
     sent = [lax.optimization_barrier(partial_value.astype(f16))]
     for k in range(1, COLS):
         sent.append(lax.ppermute(sent[0], "col", xor_pairs(COLS, k)))

time: 63.5 us -> 61.3 us (0.965)
  blocking collectives: 30.1 us -> 21.6 us
  starting transfers between devices: 9.75 us -> 14.7 us
  waiting for transfers between devices: 5.17 us -> 6.46 us
    all_gather x1 -> x0, blocking collectives: 8.5 us -> none  [local(): stats = lax.all_gather(stats, 'col')]
    ppermute x0 -> x3, starting transfers between devices: none -> 4.83 us  [local(): stats.append(lax.ppermute(stats[0], 'col', xor_pairs(COLS, k)))]
    all_to_all x1, waiting for transfers between devices: 5.15 us -> 6.17 us  [local(): every = lax.all_to_all(mine, 'row', 0, 0, tiled=True)]
  transfers between devices with their start and end apart: 7 -> 10, of which waited for: 1 -> 2; matrix products, arithmetic and copies ran while one was open for 0% -> 0% of each run, Pallas kernels for 13% -> 13%
where the time goes in v3:
time: 61.3 us; the launch traced here: 61 us
  blocking collectives  21.6 us (35%)
  Pallas kernels  14.8 us (24%)
  starting transfers between devices  14.7 us (24%)
  waiting for transfers between devices  6.46 us (11%)
  other arithmetic  1.68 us (3%)
  local copies, waits for them, and re-layouts  0.91 us (1%)
  between operations  0.78 us (1%)
    all_to_all x1, blocking collectives, local(): got = lax.all_to_all(send, 'row', 0, 0, tiled=True)  21.6 us
    pallas_call x2, Pallas kernels, written(): pl.pallas_call(functools.partial(write_kernel, first, steps), in_specs=[a...  7.06 us
    all_to_all x1, waiting for transfers between devices, local(): every = lax.all_to_all(mine, 'row', 0, 0, tiled=True)  6.17 us
    pallas_call x1, Pallas kernels, local(): pl.pallas_call(read_kernel, in_specs=[anywhere] * 8, out_specs=[vmem] * 3...  5.41 us
    ppermute x3, starting transfers between devices, local(): stats.append(lax.ppermute(stats[0], 'col', xor_pairs(COLS, k)))  4.83 us
    ppermute x3, starting transfers between devices, local(): weights.append(lax.ppermute(out_weight, 'hb', xor_pairs(HB, k)))  4.01 us
    all_to_all x1, starting transfers between devices, local(): every = lax.all_to_all(mine, 'row', 0, 0, tiled=True)  3.51 us
    ppermute x3, starting transfers between devices, local(): sent.append(lax.ppermute(sent[0], 'col', xor_pairs(COLS, k)))  2.4 us
  transfers between devices with their start and end apart: 10, of which 2 were waited for; matrix products, arithmetic and copies ran while one was open for 0% of the time, Pallas kernels for 13%

profile of v3, /device:TPU:1, one launch (start us, length us, event | category | flops | bytes accessed | tf_op | source)
XLA Modules:
  0.0 61.0 jit_solution(12157986532260097045)
XLA Ops:
  0.6 0.0 copy-start.2
  0.6 0.0 copy-start
  0.7 5.4 %read.1 = (f32[128,64]{1,0:T(8,128)}, f32[8,64]{1,0:T(8,128)}, f32[16,40,128]{2,1,0:T(8,128)}) custom-call(f32[8192,128]{1,0:T(8,128)} %bitcast.28, f32[128,64]{1,0:T(8,128)} %bitcast.35, f32[8,64]{1,0:T(8,128)} %bitcast.37, f32[128,64]{1,0:T(8,128)} %bitcast.36, f32[128,64]{1,0:T(8,128)} %bitcast.32, f32[64,8,128]{2,1,0:T(8,128)} %value_h.5, ...), custom_call_target="tpu_custom_call" | custom-call | tf_op jit(solution)/shard_map/read/pallas_call | solution.py:309
  6.1 1.0 %convert_element_type.21 = f16[16,40,128]{2,1,0:T(8,128)(2,1)S(1)} convert(f32[16,40,128]{2,1,0:T(8,128)} %get-tuple-element.12) | non-fusion elementwise | flops 81920 | bytes 491520 | tf_op jit(solution)/shard_map/convert_element_type | solution.py:366
  7.1 21.6 %all_to_all.10 = f16[16,40,128]{2,1,0:T(8,128)(2,1)S(1)} all-to-all(f16[16,40,128]{2,1,0:T(8,128)(2,1)S(1)} %convert_element_type.21), channel_id=1, replica_groups=mesh['hb'=4,'row'=16,'col'=4] {'row'}, dimensions={0} | all-to-all | bytes 327680 | tf_op jit(solution)/shard_map/all_to_all | solution.py:367
  28.7 0.9 %combine.1 = bf16[16,32,128]{2,1,0:T(8,128)(2,1)} custom-call(f32[16,40,128]{2,1,0:T(8,128)S(1)} %convert_element_type.22.got), custom_call_target="tpu_custom_call" | custom-call | tf_op jit(solution)/shard_map/combine/pallas_call | solution.py:369
  29.7 3.5 %all-to-all-start.1 = ((bf16[16,32,128]{2,1,0:T(8,128)(2,1)}), bf16[16,32,128]{2,1,0:T(8,128)(2,1)S(1)}, u32[]{:S(2)}, u32[]{:S(2)}) async-start(bf16[16,32,128]{2,1,0:T(8,128)(2,1)} %combine.1), calls=%async_computation.1 | async-start | bytes 262144 | tf_op jit(solution)/shard_map/all_to_all | solution.py:377
  33.2 1.4 %collective-permute-start.3 = (bf16[2,128,256]{2,1,0:T(8,128)(2,1)}, bf16[2,128,256]{2,1,0:T(8,128)(2,1)S(1)}, u32[]{:S(2)}, u32[]{:S(2)}) collective-permute-start(bf16[2,128,256]{2,1,0:T(8,128)(2,1)} %weight.1), channel_id=1, source_target_pairs={{0,64},{64,0},{128,192},{192,128},{1,65},{65,1},{129,193},{193,129... | collective-permute-start | bytes 393224 | tf_op jit(solution)/shard_map/ppermute | solution.py:299
  34.6 1.9 %collective-permute-start.5 = (bf16[2,128,256]{2,1,0:T(8,128)(2,1)}, bf16[2,128,256]{2,1,0:T(8,128)(2,1)S(1)}, u32[]{:S(2)}, u32[]{:S(2)}) collective-permute-start(bf16[2,128,256]{2,1,0:T(8,128)(2,1)} %weight.1), channel_id=1, source_target_pairs={{0,192},{64,128},{128,64},{192,0},{1,193},{65,129},{129,65},{193,1... | collective-permute-start | bytes 393224 | tf_op jit(solution)/shard_map/ppermute | solution.py:299
  36.5 0.7 %collective-permute-start.4 = (bf16[2,128,256]{2,1,0:T(8,128)(2,1)}, bf16[2,128,256]{2,1,0:T(8,128)(2,1)S(1)}, u32[]{:S(2)}, u32[]{:S(2)}) collective-permute-start(bf16[2,128,256]{2,1,0:T(8,128)(2,1)} %weight.1), channel_id=1, source_target_pairs={{0,128},{64,192},{128,0},{192,64},{1,129},{65,193},{129,1},{193,65... | collective-permute-start | bytes 393224 | tf_op jit(solution)/shard_map/ppermute | solution.py:299
  37.2 6.2 %all-to-all-done.1 = bf16[16,32,128]{2,1,0:T(8,128)(2,1)S(1)} async-done(((bf16[16,32,128]{2,1,0:T(8,128)(2,1)}), bf16[16,32,128]{2,1,0:T(8,128)(2,1)S(1)}, u32[]{:S(2)}, u32[]{:S(2)}) %all-to-all-start.1) | async-done | bytes 131104 | tf_op jit(solution)/shard_map/all_to_all | solution.py:377
  43.4 0.7 %stats.1 = (f32[64,8,128]{2,1,0:T(8,128)}, f32[8,128]{1,0:T(8,128)S(1)}) custom-call(bf16[512,128]{1,0:T(8,128)(2,1)S(1)} %bitcast.26), custom_call_target="tpu_custom_call" | custom-call | tf_op jit(solution)/shard_map/stats/pallas_call | solution.py:387
  44.1 3.7 %collective-permute-start.2 = (f32[8,128]{1,0:T(8,128)S(1)}, f32[8,128]{1,0:T(8,128)S(1)}, u32[]{:S(2)}, u32[]{:S(2)}) collective-permute-start(f32[8,128]{1,0:T(8,128)S(1)} %get-tuple-element.13.s0), channel_id=1, source_target_pairs={{0,3},{1,2},{2,1},{3,0},{4,7},{5,6},{6,5},{7,4},{8,11},{9,10},{10,... | collective-permute-start | bytes 12296 | tf_op jit(solution)/shard_map/ppermute | solution.py:397
  47.8 1.2 %collective-permute-start.1 = (f32[8,128]{1,0:T(8,128)S(1)}, f32[8,128]{1,0:T(8,128)S(1)}, u32[]{:S(2)}, u32[]{:S(2)}) collective-permute-start(f32[8,128]{1,0:T(8,128)S(1)} %get-tuple-element.13.s0), channel_id=1, source_target_pairs={{0,2},{1,3},{2,0},{3,1},{4,6},{5,7},{6,4},{7,5},{8,10},{9,11},{10,... | collective-permute-start | bytes 12296 | tf_op jit(solution)/shard_map/ppermute | solution.py:397
  48.9 0.0 collective-permute-done.3.w1
  49.0 0.0 collective-permute-start
  49.0 0.0 copy-done.2
  49.0 0.0 copy-done
  49.0 0.0 copy-start.1
  49.0 0.9 %copy-done.1 = bf16[2,128,256]{2,1,0:T(8,128)(2,1)S(1)} copy-done((bf16[2,128,256]{2,1,0:T(8,128)(2,1)S(1)}, bf16[2,128,256]{2,1,0:T(8,128)(2,1)}, u32[]{:S(2)}) %copy-start.1) | copy-done | bytes 131096
  49.9 0.1 gate.1
  50.0 0.0 collective-permute-done.5.w3
  50.0 0.0 collective-permute-done.4.w2
  50.0 0.0 collective-permute-done.2.s3
  50.0 0.3 collective-permute-done.1.s2
  50.3 0.0 collective-permute-done.s1
  50.3 0.6 project.1
  50.9 1.2 %collective-permute-start.8 = (f16[64,256]{1,0:T(8,128)(2,1)S(1)}, f16[64,256]{1,0:T(8,128)(2,1)S(1)}, u32[]{:S(2)}, u32[]{:S(2)}) collective-permute-start(f16[64,256]{1,0:T(8,128)(2,1)S(1)} %convert_element_type.23), channel_id=1, source_target_pairs={{0,3},{1,2},{2,1},{3,0},{4,7},{5,6},{6,5},{7,4},{8,11},{9,10},{10,... | collective-permute-start | bytes 98312 | tf_op jit(solution)/shard_map/ppermute | solution.py:410
  52.1 1.2 %collective-permute-start.7 = (f16[64,256]{1,0:T(8,128)(2,1)S(1)}, f16[64,256]{1,0:T(8,128)(2,1)S(1)}, u32[]{:S(2)}, u32[]{:S(2)}) collective-permute-start(f16[64,256]{1,0:T(8,128)(2,1)S(1)} %convert_element_type.23), channel_id=1, source_target_pairs={{0,2},{1,3},{2,0},{3,1},{4,6},{5,7},{6,4},{7,5},{8,10},{9,11},{10,... | collective-permute-start | bytes 98312 | tf_op jit(solution)/shard_map/ppermute | solution.py:410
  53.3 0.0 collective-permute-start.6
  53.3 4.5 %shard_map.146.rest_0_ = f32[8192,128]{1,0:T(8,128)} custom-call(f32[8192,128]{1,0:T(8,128)} %bitcast.29, f32[8,64]{1,0:T(8,128)} %bitcast.38, f32[128,64]{1,0:T(8,128)} %bitcast.33, f32[64,8,128]{2,1,0:T(8,128)} %value_h.5, f32[8,64]{1,0:T(8,128)} %bitcast.41, f32[8,64]{1,0:T(8,128)} %bitcast.44), custom_call_target="tpu_custom_call" | custom-call | bytes 6291456 | tf_op jit(solution)/shard_map/pallas_call | solution.py:340
  57.7 2.6 %shard_map.147 = f32[8192,128]{1,0:T(8,128)} custom-call(f32[8192,128]{1,0:T(8,128)} %bitcast.30, f32[8,64]{1,0:T(8,128)} %bitcast.39, f32[128,64]{1,0:T(8,128)} %bitcast.34, f32[64,8,128]{2,1,0:T(8,128)} %value_h.5, f32[8,64]{1,0:T(8,128)} %bitcast.42, f32[8,64]{1,0:T(8,128)} %bitcast.45, ...), custom_call_target="tpu_custom_call", output_to_operand_aliasing={{}: (6, {})} | custom-call | bytes 2097152 | tf_op jit(solution)/shard_map/pallas_call | solution.py:340
  60.4 0.0 collective-permute-done.8
  60.4 0.0 collective-permute-done.7
  60.4 0.0 collective-permute-done.6
  60.4 0.7 %add_multiply_fusion = f32[64,256]{1,0:T(8,128)} fusion(f16[64,256]{1,0:T(8,128)(2,1)S(1)} %collective-permute-done.8, f16[64,256]{1,0:T(8,128)(2,1)S(1)} %collective-permute-done.7, f16[64,256]{1,0:T(8,128)(2,1)S(1)} %collective-permute-done.6, f16[64,256]{1,0:T(8,128)(2,1)S(1)} %convert_element_type.23), kind=kLoop, calls=%fused_computation | loop fusion | flops 131072 | bytes 196608 | tf_op jit(solution)/shard_map/mul | solution.py:412
  (2 shorter events, 0.0 us)
Async XLA Ops:
  0.6 48.3 %copy-start.2 = (f32[8,128]{1,0:T(8,128)S(1)}, f32[8,128]{1,0:T(8,128)}, u32[]{:S(2)}) copy-start(f32[8,128]{1,0:T(8,128)} %gain.1) | copy-start | bytes 12292
  0.6 48.3 %copy-start = (f32[64,8,128]{2,1,0:T(8,128)S(1)}, f32[64,8,128]{2,1,0:T(8,128)}, u32[]{:S(2)}) copy-start(f32[64,8,128]{2,1,0:T(8,128)} %logits.1) | copy-start | bytes 786436
  29.7 13.7 %all-to-all-start.1 = ((bf16[16,32,128]{2,1,0:T(8,128)(2,1)}), bf16[16,32,128]{2,1,0:T(8,128)(2,1)S(1)}, u32[]{:S(2)}, u32[]{:S(2)}) async-start(bf16[16,32,128]{2,1,0:T(8,128)(2,1)} %combine.1), calls=%async_computation.1 | async-start | bytes 262144 | tf_op jit(solution)/shard_map/all_to_all | solution.py:377
  33.2 15.7 %collective-permute-start.3 = (bf16[2,128,256]{2,1,0:T(8,128)(2,1)}, bf16[2,128,256]{2,1,0:T(8,128)(2,1)S(1)}, u32[]{:S(2)}, u32[]{:S(2)}) collective-permute-start(bf16[2,128,256]{2,1,0:T(8,128)(2,1)} %weight.1), channel_id=1, source_target_pairs={{0,64},{64,0},{128,192},{192,128},{1,65},{65,1},{129,193},{193,129... | collective-permute-start | bytes 393224 | tf_op jit(solution)/shard_map/ppermute | solution.py:299
  34.6 15.4 %collective-permute-start.5 = (bf16[2,128,256]{2,1,0:T(8,128)(2,1)}, bf16[2,128,256]{2,1,0:T(8,128)(2,1)S(1)}, u32[]{:S(2)}, u32[]{:S(2)}) collective-permute-start(bf16[2,128,256]{2,1,0:T(8,128)(2,1)} %weight.1), channel_id=1, source_target_pairs={{0,192},{64,128},{128,64},{192,0},{1,193},{65,129},{129,65},{193,1... | collective-permute-start | bytes 393224 | tf_op jit(solution)/shard_map/ppermute | solution.py:299
  36.5 13.5 %collective-permute-start.4 = (bf16[2,128,256]{2,1,0:T(8,128)(2,1)}, bf16[2,128,256]{2,1,0:T(8,128)(2,1)S(1)}, u32[]{:S(2)}, u32[]{:S(2)}) collective-permute-start(bf16[2,128,256]{2,1,0:T(8,128)(2,1)} %weight.1), channel_id=1, source_target_pairs={{0,128},{64,192},{128,0},{192,64},{1,129},{65,193},{129,1},{193,65... | collective-permute-start | bytes 393224 | tf_op jit(solution)/shard_map/ppermute | solution.py:299
  44.1 5.9 %collective-permute-start.2 = (f32[8,128]{1,0:T(8,128)S(1)}, f32[8,128]{1,0:T(8,128)S(1)}, u32[]{:S(2)}, u32[]{:S(2)}) collective-permute-start(f32[8,128]{1,0:T(8,128)S(1)} %get-tuple-element.13.s0), channel_id=1, source_target_pairs={{0,3},{1,2},{2,1},{3,0},{4,7},{5,6},{6,5},{7,4},{8,11},{9,10},{10,... | collective-permute-start | bytes 12296 | tf_op jit(solution)/shard_map/ppermute | solution.py:397
  47.8 2.5 %collective-permute-start.1 = (f32[8,128]{1,0:T(8,128)S(1)}, f32[8,128]{1,0:T(8,128)S(1)}, u32[]{:S(2)}, u32[]{:S(2)}) collective-permute-start(f32[8,128]{1,0:T(8,128)S(1)} %get-tuple-element.13.s0), channel_id=1, source_target_pairs={{0,2},{1,3},{2,0},{3,1},{4,6},{5,7},{6,4},{7,5},{8,10},{9,11},{10,... | collective-permute-start | bytes 12296 | tf_op jit(solution)/shard_map/ppermute | solution.py:397
  49.0 1.3 %collective-permute-start = (f32[8,128]{1,0:T(8,128)S(1)}, f32[8,128]{1,0:T(8,128)S(1)}, u32[]{:S(2)}, u32[]{:S(2)}) collective-permute-start(f32[8,128]{1,0:T(8,128)S(1)} %get-tuple-element.13.s0), channel_id=1, source_target_pairs={{0,1},{1,0},{2,3},{3,2},{4,5},{5,4},{6,7},{7,6},{8,9},{9,8},{10,11... | collective-permute-start | bytes 12296 | tf_op jit(solution)/shard_map/ppermute | solution.py:397
  49.0 0.9 %copy-start.1 = (bf16[2,128,256]{2,1,0:T(8,128)(2,1)S(1)}, bf16[2,128,256]{2,1,0:T(8,128)(2,1)}, u32[]{:S(2)}) copy-start(bf16[2,128,256]{2,1,0:T(8,128)(2,1)} %weight.1) | copy-start | bytes 393220
  50.9 9.5 %collective-permute-start.8 = (f16[64,256]{1,0:T(8,128)(2,1)S(1)}, f16[64,256]{1,0:T(8,128)(2,1)S(1)}, u32[]{:S(2)}, u32[]{:S(2)}) collective-permute-start(f16[64,256]{1,0:T(8,128)(2,1)S(1)} %convert_element_type.23), channel_id=1, source_target_pairs={{0,3},{1,2},{2,1},{3,0},{4,7},{5,6},{6,5},{7,4},{8,11},{9,10},{10,... | collective-permute-start | bytes 98312 | tf_op jit(solution)/shard_map/ppermute | solution.py:410
  52.1 8.3 %collective-permute-start.7 = (f16[64,256]{1,0:T(8,128)(2,1)S(1)}, f16[64,256]{1,0:T(8,128)(2,1)S(1)}, u32[]{:S(2)}, u32[]{:S(2)}) collective-permute-start(f16[64,256]{1,0:T(8,128)(2,1)S(1)} %convert_element_type.23), channel_id=1, source_target_pairs={{0,2},{1,3},{2,0},{3,1},{4,6},{5,7},{6,4},{7,5},{8,10},{9,11},{10,... | collective-permute-start | bytes 98312 | tf_op jit(solution)/shard_map/ppermute | solution.py:410
  53.3 7.1 %collective-permute-start.6 = (f16[64,256]{1,0:T(8,128)(2,1)S(1)}, f16[64,256]{1,0:T(8,128)(2,1)S(1)}, u32[]{:S(2)}, u32[]{:S(2)}) collective-permute-start(f16[64,256]{1,0:T(8,128)(2,1)S(1)} %convert_element_type.23), channel_id=1, source_target_pairs={{0,1},{1,0},{2,3},{3,2},{4,5},{5,4},{6,7},{7,6},{8,9},{9,8},{10,11... | collective-permute-start | bytes 98312 | tf_op jit(solution)/shard_map/ppermute | solution.py:410
